TPU v7x, 256 devices: a whole 4x4x8 slice. The times are simulated.
256 devices in a mesh: dp: 128 (over x_lo, z, y, core), space: 2 (over x_hi).
Axes of the slice: x: 4 (x_hi: 2, x_lo: 2; x = x_hi * 2 + x_lo), y: 4, z: 8, core: 2. Of those that a mesh axis runs over, the one named last changes fastest.
Arguments:
- feature_map: bfloat16 [128, 24, 84, 256], P('dp', 'space'), may hold values from -6 to 6
- proposals: int32 [128, 128, 4], P('dp'), may hold values from 0 to 84, as said below
- hidden_weight: bfloat16 [12544, 512], P(None, 'space'), may hold values from -0.0546875 to 0.0546875
- output_weight: bfloat16 [512, 512], P('space'), may hold values from -0.25 to 0.25
- upstream: bfloat16 [128, 128, 512], P('dp'), may hold values from -6 to 6
Outputs:
- hidden_weight_grad: float32 [12544, 512], P('dp', 'space')
- output_weight_grad: float32 [512, 512], P('space')
- feature_grad: float32 [128, 24, 84, 256], P('dp', 'space')
Inputs may be any that keep to these rules, and one draw needn't show every extreme that they name: `proposals`: each row holds top, left, bottom, right with top < bottom <= 24 and left < right <= 84.
All inputs are finite; a program needn't handle non-finite values.
Results may differ from a plain program's by a relative error of at most 0.012.
Values may be sent and summed in bfloat16 or wider, within the bound.
A program may use at most 128 MiB of HBM per device.

v0:
```python
import jax
import jax.numpy as jnp
from jax import lax
from jax.sharding import PartitionSpec as P

POOL = 7


def copy_for_each(x, axis):
    size = lax.axis_size(axis)
    return lax.all_to_all(jnp.broadcast_to(x[None], (size, *x.shape)), axis, 0, 0, tiled=True)


def joined_along(blocks, dim):
    blocks = jnp.moveaxis(blocks, 0, dim)
    dims = blocks.shape
    return blocks.reshape(*dims[:dim], dims[dim] * dims[dim + 1], *dims[dim + 2 :])


def collect(x, axis, dim):
    blocks = copy_for_each(x, axis)
    return joined_along(blocks, dim)


def over_copies(x, axis):
    return copy_for_each(x, axis).astype(jnp.float32).sum(axis=0)


def in_blocks(x, dim, size):
    before, after = (x.shape[:dim], x.shape[dim + 1 :])
    return jnp.moveaxis(x.reshape(*before, size, -1, *after), dim, 0)


def summed_on_arrival(x, axis, dim):
    blocks = in_blocks(x, dim, lax.axis_size(axis))
    arrived = lax.all_to_all(blocks, axis, split_axis=0, concat_axis=0, tiled=True)
    return arrived.astype(jnp.float32).sum(axis=0)


def axis_weights(low_edge, high_edge, grid_points):
    edge_start = low_edge.astype(jnp.float32)
    bin_size = (high_edge - low_edge).astype(jnp.float32) / POOL
    bin_index = jnp.arange(POOL).astype(jnp.float32)
    offsets = jnp.array([0.25, 0.75], jnp.float32)
    sample_points = (
        edge_start[:, None, None]
        + (bin_index[None, :, None] + offsets[None, None, :]) * bin_size[:, None, None]
        - 0.5
    )
    weights = jnp.maximum(
        0.0, 1.0 - jnp.abs(sample_points[..., None] - grid_points[None, None, None, :])
    )
    return jnp.mean(weights, axis=2)


def activate(values):
    return jax.nn.gelu(values, approximate=True)


def gelu_grad(values, incoming):
    return jax.vjp(activate, values)[1](incoming)[0]


def block_shape(proposal_count):
    block_size = 32
    return (block_size, proposal_count // block_size)


def crop_rows(own_map, row_weight, col_weight):
    height_cells, width_cells, channels = own_map.shape
    proposal_count = row_weight.shape[0]
    block_size, block_count = block_shape(proposal_count)
    flattened = jnp.transpose(own_map, (1, 0, 2)).reshape(width_cells, height_cells * channels)

    def per_block(blocks):
        row_part, col_part = blocks
        across = jnp.dot(
            col_part.reshape(block_size * POOL, width_cells),
            flattened,
            preferred_element_type=jnp.float32,
        )
        across = across.reshape(block_size, POOL, height_cells, channels)
        return jnp.einsum("riy,rjyc->rijc", row_part, across, precision=lax.Precision.HIGHEST)

    pooled = lax.map(
        per_block,
        (
            row_weight.reshape(block_count, block_size, POOL, height_cells),
            col_weight.reshape(block_count, block_size, POOL, width_cells),
        ),
    )
    return pooled.reshape(proposal_count, POOL * POOL * channels)


def crop_back(grad_pooled, row_weight, col_weight, channels):
    proposal_count, _, height_cells = row_weight.shape
    width_cells = col_weight.shape[2]
    block_size, block_count = block_shape(proposal_count)

    def per_block(running, blocks):
        row_part, col_part, grad_part = blocks
        grad_block = grad_part.reshape(block_size, POOL, POOL, channels)
        spread = jnp.einsum("riy,rijc->rjyc", row_part, grad_block, precision=lax.Precision.HIGHEST)
        added = lax.dot_general(
            col_part.astype(jnp.float32).reshape(block_size * POOL, width_cells),
            spread.reshape(block_size * POOL, height_cells * channels),
            (((0,), (0,)), ((), ())),
            precision=lax.Precision.HIGHEST,
            preferred_element_type=jnp.float32,
        )
        return (running + added, None)

    start = jnp.zeros((width_cells, height_cells * channels), jnp.float32)
    blocks = (
        row_weight.reshape(block_count, block_size, POOL, height_cells),
        col_weight.reshape(block_count, block_size, POOL, width_cells),
        grad_pooled.reshape(block_count, block_size, grad_pooled.shape[1]),
    )
    total, _ = lax.scan(per_block, start, blocks)
    return jnp.transpose(total.reshape(width_cells, height_cells, channels), (1, 0, 2))


def on_device(feature_map, proposals, hidden_weight, output_weight, upstream):
    own_map = feature_map[0]
    corners = proposals[0]
    own_height = own_map.shape[0]
    map_width = own_map.shape[1]
    channels = own_map.shape[2]
    col_weight = axis_weights(
        corners[:, 1], corners[:, 3], jnp.arange(map_width, dtype=jnp.int32).astype(jnp.float32)
    ).astype(jnp.bfloat16)
    full_grid = jnp.arange(own_height * lax.axis_size("space"), dtype=jnp.int32).astype(jnp.float32)
    full_weight = axis_weights(corners[:, 0], corners[:, 2], full_grid)
    whole_map = collect(own_map, "space", 0)
    pooled = crop_rows(whole_map, full_weight, col_weight).astype(jnp.bfloat16)
    pre_hidden = jnp.dot(pooled, hidden_weight, preferred_element_type=jnp.float32)
    hidden = activate(pre_hidden).astype(jnp.bfloat16)
    pre_output = over_copies(
        jnp.dot(hidden, output_weight, preferred_element_type=jnp.float32).astype(jnp.bfloat16),
        "space",
    ).astype(jnp.float32)
    output_delta = gelu_grad(pre_output, upstream[0].astype(jnp.float32)).astype(jnp.bfloat16)
    step_second = lax.dot_general(
        hidden, output_delta, (((0,), (0,)), ((), ())), preferred_element_type=jnp.float32
    )
    second_total = lax.psum(step_second, "dp")
    hidden_back = lax.dot_general(
        output_delta, output_weight, (((1,), (1,)), ((), ())), preferred_element_type=jnp.float32
    )
    hidden_delta = gelu_grad(pre_hidden, hidden_back).astype(jnp.bfloat16)
    step_first = lax.dot_general(
        pooled, hidden_delta, (((0,), (0,)), ((), ())), preferred_element_type=jnp.float32
    )
    first_total = lax.psum_scatter(step_first, "dp", scatter_dimension=0, tiled=True)
    partial_grad = lax.dot_general(
        hidden_delta, hidden_weight, (((1,), (1,)), ((), ())), preferred_element_type=jnp.float32
    )
    whole_grad = crop_back(partial_grad, full_weight, col_weight, channels)
    map_grad = summed_on_arrival(whole_grad.astype(jnp.bfloat16), "space", 0)
    return (first_total, second_total, map_grad[None])


def solution(mesh):
    placed = (
        P("dp", "space", None, None),
        P("dp", None, None),
        P(None, "space"),
        P("space", None),
        P("dp", None, None),
    )
    return jax.shard_map(
        on_device,
        mesh=mesh,
        in_specs=placed,
        out_specs=(P("dp", "space"), P("space", None), P("dp", "space", None, None)),
        check_vma=False,
    )
```

profile of v0, /device:TPU:1, one launch (start us, length us, event | category | flops | bytes accessed | tf_op | source)
XLA Modules:
  0.0 1233.8 jit_solution(13362167307446305481)
XLA Ops:
  9.4 4.8 all-to-all-start
  16.4 11.4 all-to-all-done
  28.3 34.8 %while.21 = (s32[]{:T(128)}, bf16[4,32,7,7,256]{4,2,3,1,0:T(8,128)(2,1)}, f32[4,32,7,24]{3,2,1,0:T(8,128)S(1)}, bf16[4,32,7,84]{3,1,0,2:T(8,128)(2,1)S(1)}, bf16[84,6144]{1,0:T(8,128)(2,1)S(1)}, /*index=5*/s32[]{:T(128)}) while((s32[]{:T(128)}, bf16[4,32,7,7,256]{4,2,3,1,0:T(8,128)(2,1)}, f32[4,32,7,24]{3,2,1,0:T(8,128)S(1)}, ...), condition=%wide.region_3.4_spmd, body=%wide.region_2.3_spmd.sunk | while | flops 346816512 | bytes 18293832 | solution.py:85
  29.7 7.5 bitcast_dynamic-update-slice_fusion.2
  38.3 7.5 bitcast_dynamic-update-slice_fusion.2
  47.0 7.5 bitcast_dynamic-update-slice_fusion.2
  55.6 7.4 bitcast_dynamic-update-slice_fusion.2
  63.9 5.2 copy.44
  69.1 5.6 convert_element_type.119
  74.7 3.8 fusion.37
  80.1 4.3 all-to-all-start.1
  86.2 3.6 all-to-all-done.1
  93.4 6.5 fusion.38
  99.9 4.9 fusion.39
  105.8 91.8 %while.22 = (s32[]{:T(128)}, f32[84,6144]{1,0:T(8,128)}, bf16[4,32,7,84]{3,2,1,0:T(8,128)(2,1)}, f32[4,32,12544]{2,1,0:T(8,128)}, f32[4,32,7,24]{3,2,1,0:T(8,128)}, /*index=5*/s32[]{:T(128)}, s32[]{:T(128)}) while((s32[]{:T(128)}, f32[84,6144]{1,0:T(8,128)}, bf16[4,32,7,84]{3,2,1,0:T(8,128)(2,1)}, f32[4,32,12544]{2,1,0:T(8,128)}, ...), condition=%wide.region_8.9_spmd.clone, body=%wide.region_7.8_spmd.clone.sunk | while | flops 1503903744 | bytes 51011988 | solution.py:119
  105.8 2.7 constant_dynamic-slice_fusion.6
  110.3 5.7 fusion.71
  116.0 4.6 copy.77
  121.5 5.9 convolution_add_fusion.2
  133.2 5.7 fusion.71
  139.0 4.6 copy.77
  144.4 5.9 convolution_add_fusion.2
  156.2 5.7 fusion.71
  161.9 4.6 copy.77
  167.4 5.9 convolution_add_fusion.2
  179.1 5.7 fusion.71
  184.9 4.6 copy.77
  190.3 5.9 convolution_add_fusion.2
  200.9 3.6 all-to-all-start.2
  205.2 326.5 %fusion = f32[104,256]{1,0:T(8,128)S(1)} fusion(f32[12544,256]{1,0:T(8,128)} %fusion.38), kind=kCustom, calls=%all-reduce-scatter | all-reduce-scatter fusion | flops 3407873 | bytes 12952576
  541.8 8.9 collective-permute-start.6
  556.4 668.7 %all-reduce.4.cloned.1.call-done = f32[256,512]{1,0:T(8,128)} async-done(((f32[256,512]{1,0:T(8,128)}), f32[256,512]{1,0:T(8,128)}) %all-reduce.4.cloned.1.call-update) | async-done | bytes 524304 | tf_op jit(solution)/shard_map/psum | solution.py:146
  (121 shorter events, 63.3 us)
Async XLA Ops:
  7.2 72.0 %copy-start = (bf16[256,512]{1,0:T(8,128)(2,1)S(1)}, bf16[256,512]{1,0:T(8,128)(2,1)}, u32[]{:S(2)}) copy-start(bf16[256,512]{1,0:T(8,128)(2,1)} %param.14) | copy-start | bytes 786436
  7.2 7.1 copy-start.9
  7.2 7.0 copy-start.8
  9.4 18.4 %all-to-all-start = ((bf16[2,12,84,256]{3,2,1,0:T(8,128)(2,1)}), bf16[2,12,84,256]{3,2,1,0:T(8,128)(2,1)S(1)}, u32[]{:S(2)}, u32[]{:S(2)}) async-start(bf16[2,12,84,256]{3,2,1,0:T(8,128)(2,1)} %broadcast_in_dim.17), calls=%async_computation | async-start | bytes 2162688 | tf_op jit(solution)/shard_map/all_to_all | solution.py:11
  15.5 0.7 copy-start.5
  63.1 0.8 copy-start.4
  78.5 0.7 copy-start.6
  80.1 9.7 all-to-all-start.1
  89.8 10.1 slice-start
  93.4 6.5 slice-start.1
  99.9 4.9 copy-start.7
  116.0 5.5 copy-start.2
  127.4 1.4 copy-start.3
  139.0 5.5 copy-start.2
  150.3 1.4 copy-start.3
  161.9 5.5 copy-start.2
  173.2 1.4 copy-start.3
  184.9 5.5 copy-start.2
  196.2 1.4 copy-start.3
  200.9 353.7 %all-to-all-start.2 = ((bf16[2,12,84,256]{3,2,1,0:T(8,128)(2,1)}), bf16[2,12,84,256]{3,2,1,0:T(8,128)(2,1)S(1)}, u32[]{:S(2)}, u32[]{:S(2)}) async-start(bf16[2,12,84,256]{3,2,1,0:T(8,128)(2,1)} %bitcast.23), calls=%async_computation.2 | async-start | bytes 2162688 | tf_op jit(solution)/shard_map/all_to_all | solution.py:36
  204.5 1020.6 %all-reduce.4.cloned.1.call-start = ((), (), s32[]{:S(2)}) async-start(), calls=%async_computation.3 | async-start | bytes 1048576 | tf_op jit(solution)/shard_map/psum | solution.py:146
  205.2 345.5 %copy-start.10 = (u32[256]{0:T(256)S(1)}, u32[256]{0:T(256)}, u32[]{:S(2)}) copy-start(u32[256]{0:T(256)} %constant.68) | copy-start | bytes 3076
  531.7 8.7 collective-permute-start
  533.9 7.9 collective-permute-start.1
  535.2 3.9 collective-permute-start.7
  536.5 15.4 %collective-permute-start.2 = (f32[104,256]{1,0:T(8,128)S(1)}, f32[104,256]{1,0:T(8,128)S(1)}, u32[]{:S(2)}, u32[]{:S(2)}) collective-permute-start(f32[104,256]{1,0:T(8,128)S(1)} %fusion), channel_id=1, source_target_pairs={{0,6},{2,8},{4,10},{6,12},{8,14},{10,16},{12,18},{14,20},{16,22},{... | collective-permute-start | bytes 319496
  537.8 14.1 %collective-permute-start.3 = (f32[104,256]{1,0:T(8,128)S(1)}, f32[104,256]{1,0:T(8,128)S(1)}, u32[]{:S(2)}, u32[]{:S(2)}) collective-permute-start(f32[104,256]{1,0:T(8,128)S(1)} %fusion), channel_id=1, source_target_pairs={{0,8},{2,10},{4,12},{6,14},{8,16},{10,18},{12,20},{14,22},{16,24},... | collective-permute-start | bytes 319496
  539.1 12.8 %collective-permute-start.4 = (f32[104,256]{1,0:T(8,128)S(1)}, f32[104,256]{1,0:T(8,128)S(1)}, u32[]{:S(2)}, u32[]{:S(2)}) collective-permute-start(f32[104,256]{1,0:T(8,128)S(1)} %fusion), channel_id=1, source_target_pairs={{0,10},{2,12},{4,14},{6,16},{8,18},{10,20},{12,22},{14,24},{16,26}... | collective-permute-start | bytes 319496
  540.4 11.5 collective-permute-start.5
  541.8 10.6 collective-permute-start.6
  552.4 674.6 %copy-start.1 = (bf16[256,512]{1,0:T(8,128)(2,1)S(1)}, bf16[256,512]{1,0:T(8,128)(2,1)}, u32[]{:S(2)}) copy-start(bf16[256,512]{1,0:T(8,128)(2,1)} %param.14) | copy-start | bytes 786436
Sparse Core Ops, SparseCore 0:
  208.5 1016.5 all-reduce.3
where the time goes:
time: 1240 us; the launch traced here: 1230 us
  waiting for transfers between devices  685 us (55%)
  blocking collectives  327 us (26%)
  matrix products  97.2 us (8%)
  local copies, waits for them, and re-layouts  72.4 us (6%)
  starting transfers between devices  31.6 us (3%)
  between operations  15.1 us (1%)
    psum x1, waiting for transfers between devices, on_device(): second_total = lax.psum(step_second, 'dp')  669 us
    unnamed x1, blocking collectives  327 us
    dot_general x4, matrix products, per_block(): jnp.einsum('riy,rjyc->rijc', row_part, across, precision=lax.Precision.HI...  29.8 us
    while x24, local copies, waits for them, and re-layouts  24.8 us
  transfers between devices with their start and end apart: 12, of which 4 were waited for; matrix products, arithmetic and copies ran while one was open for 27% of the time, Pallas kernels for 0%

commit v1 on v0

--- a/solution.py
+++ b/solution.py
@@ -1,8 +1,11 @@
 import jax
 import jax.numpy as jnp
 from jax import lax
+from jax.experimental import pallas as pl
+from jax.experimental.pallas import tpu as pltpu
 from jax.sharding import PartitionSpec as P
 
+MESH = pl.DeviceIdType.MESH
 POOL = 7
 
 
@@ -118,6 +121,195 @@
     )
     total, _ = lax.scan(per_block, start, blocks)
     return jnp.transpose(total.reshape(width_cells, height_cells, channels), (1, 0, 2))
+
+
+def place():
+    me = lax.axis_index("dp")
+    return me // 64, (me // 8) % 8, (me // 2) % 4, me % 2
+
+
+def index_of(x, z, y, c):
+    return ((x * 8 + z) * 4 + y) * 2 + c
+
+
+def chains_of(hops):
+    return ((0, 1, hops), (1, -1, hops), (0, -1, hops - 1), (1, 1, hops - 1))
+
+
+def reduce_kernel(
+    s_ref, first_ref, second_ref,
+    za_s, za_r, yb_s, yb_r, ya_s, ya_r, zb_s, zb_r, x_s, x_r, c_s, c_r, gather,
+    acc_a, acc_b, mid_a, mid_b, final,
+    za_ss, za_rs, yb_ss, yb_rs, ya_ss, ya_rs, zb_ss, zb_rs, xc_ss, xc_rs, g_ss, g_rs,
+):
+    x, z, y, c = place()
+
+    def at_z(step):
+        return {"dp": index_of(x, (z + step + 8) % 8, y, c)}
+
+    def at_y(step):
+        return {"dp": index_of(x, z, (y + step + 4) % 4, c)}
+
+    at_x = {"dp": index_of(1 - x, z, y, c)}
+    at_c = {"dp": index_of(x, z, y, 1 - c)}
+
+    barrier = pltpu.get_barrier_semaphore()
+    peers = [at_z(k) for k in range(1, 8)] + [at_y(k) for k in range(1, 4)] + [at_x, at_c]
+    for peer in peers:
+        pl.semaphore_signal(barrier, inc=1, device_id=peer, device_id_type=MESH)
+    pl.semaphore_wait(barrier, len(peers))
+
+    copies = []
+
+    def ring(size, pos, to, own, send, recv, ssem, rsem):
+        chains = chains_of(size // 2)
+        live = {}
+
+        def slot(k, h):
+            return sum(ch[2] for ch in chains[:k]) + h
+
+        def go(k, h):
+            u, way, hops = chains[k]
+            if h > 0:
+                live[k, h - 1].wait_recv()
+            dest = (pos + way * (hops - h) + size) % size
+            value = own(u, dest)
+            if h > 0:
+                value = value + recv[slot(k, h - 1)].astype(jnp.float32)
+            at = slot(k, h)
+            send[at] = value.astype(jnp.bfloat16)
+            live[k, h] = pltpu.make_async_remote_copy(
+                src_ref=send.at[at], dst_ref=recv.at[at], send_sem=ssem.at[at], recv_sem=rsem.at[at],
+                device_id=to(way), device_id_type=MESH,
+            )
+            live[k, h].start()
+            copies.append(live[k, h])
+
+        def total(u):
+            value = own(u, pos)
+            for k, (piece, _, hops) in enumerate(chains):
+                if piece == u and hops > 0:
+                    live[k, hops - 1].wait_recv()
+                    value = value + recv[slot(k, hops - 1)].astype(jnp.float32)
+            return value
+
+        return go, total
+
+    za_go, za_total = ring(8, z, at_z, lambda u, d: s_ref[u, d, :, 0:96, :], za_s, za_r, za_ss, za_rs)
+    yb_go, yb_total = ring(4, y, at_y, lambda u, d: s_ref[u, :, d, 96:208, :], yb_s, yb_r, yb_ss, yb_rs)
+    ya_go, ya_total = ring(4, y, at_y, lambda u, d: acc_a[u, d], ya_s, ya_r, ya_ss, ya_rs)
+    zb_go, zb_total = ring(8, z, at_z, lambda u, d: acc_b[u, d], zb_s, zb_r, zb_ss, zb_rs)
+
+    for k in (0, 1):
+        za_go(k, 0)
+    for k in (0, 1):
+        yb_go(k, 0)
+    for k in (2, 3):
+        za_go(k, 0)
+    for k in (2, 3):
+        yb_go(k, 0)
+    for k in (0, 1, 2, 3):
+        za_go(k, 1)
+    for k in (0, 1):
+        yb_go(k, 1)
+    for k in (0, 1, 2, 3):
+        za_go(k, 2)
+    for k in (0, 1):
+        za_go(k, 3)
+    for u in (0, 1):
+        acc_a[u] = za_total(u)
+        ya_go(u, 0)
+    for k in (2, 3):
+        ya_go(k, 0)
+    for u in (0, 1):
+        acc_b[u] = yb_total(u)
+        zb_go(u, 0)
+    for k in (2, 3):
+        zb_go(k, 0)
+    for k in (0, 1):
+        ya_go(k, 1)
+    for k in (0, 1, 2, 3):
+        zb_go(k, 1)
+    for u in (0, 1):
+        mid_a[u] = ya_total(u)
+    for k in (0, 1, 2, 3):
+        zb_go(k, 2)
+    for k in (0, 1):
+        zb_go(k, 3)
+    for u in (0, 1):
+        mid_b[u] = zb_total(u)
+
+    def one(src, dst, ssem, rsem, peer):
+        copy = pltpu.make_async_remote_copy(
+            src_ref=src, dst_ref=dst, send_sem=ssem, recv_sem=rsem, device_id=peer, device_id_type=MESH
+        )
+        copy.start()
+        copies.append(copy)
+        return copy
+
+    x_s[0:96] = mid_a[1 - x].astype(jnp.bfloat16)
+    x_s[96:208] = mid_b[1 - x].astype(jnp.bfloat16)
+    across = one(x_s, x_r, xc_ss.at[0], xc_rs.at[0], at_x)
+    across.wait_recv()
+    final[0:96] = mid_a[x] + x_r[0:96].astype(jnp.float32)
+    final[96:208] = mid_b[x] + x_r[96:208].astype(jnp.float32)
+
+    gather[c, x, z, y] = final[0:8]
+    mine = gather.at[c, x, z, y]
+    steps = [one(mine, mine, g_ss.at[k], g_rs.at[k], at_z(k)) for k in range(1, 8)]
+    low, high = final[8:106], final[106:204]
+    c_s[...] = jnp.where(c == 0, high, low)
+    swap = one(c_s, c_r, xc_ss.at[1], xc_rs.at[1], at_c)
+    swap.wait_recv()
+    kept = jnp.where(c == 0, low, high)
+    got = c_r[...]
+    first_ref[:, 0:128] = jnp.where(c == 0, kept, got)
+    first_ref[:, 128:256] = jnp.where(c == 0, got, kept)
+    for step in steps:
+        step.wait_recv()
+    steps = []
+    for k in range(1, 4):
+        column = gather.at[c, x, :, y]
+        steps.append(one(column, column, g_ss.at[7 + k], g_rs.at[7 + k], at_y(k)))
+    for step in steps:
+        step.wait_recv()
+    plane = gather.at[c, x]
+    one(plane, plane, g_ss.at[11], g_rs.at[11], at_x).wait_recv()
+    half = gather.at[c]
+    one(half, half, g_ss.at[12], g_rs.at[12], at_c).wait_recv()
+    for k in range(2):
+        for u in range(2):
+            at = k * 256 + u * 128
+            second_ref[:, at:at + 128] = gather[k, u].reshape(256, 128)
+    for copy in copies:
+        copy.wait_send()
+
+
+def reduce_all(s):
+    bf, f32 = jnp.bfloat16, jnp.float32
+    dma = pltpu.SemaphoreType.DMA
+    return pl.pallas_call(
+        reduce_kernel,
+        out_shape=(jax.ShapeDtypeStruct((98, 256), f32), jax.ShapeDtypeStruct((256, 512), f32)),
+        in_specs=[pl.BlockSpec(memory_space=pltpu.VMEM)],
+        out_specs=[pl.BlockSpec(memory_space=pltpu.VMEM)] * 2,
+        scratch_shapes=[
+            pltpu.VMEM((14, 4, 96, 128), bf), pltpu.VMEM((14, 4, 96, 128), bf),
+            pltpu.VMEM((6, 8, 112, 128), bf), pltpu.VMEM((6, 8, 112, 128), bf),
+            pltpu.VMEM((6, 96, 128), bf), pltpu.VMEM((6, 96, 128), bf),
+            pltpu.VMEM((14, 112, 128), bf), pltpu.VMEM((14, 112, 128), bf),
+            pltpu.VMEM((208, 128), bf), pltpu.VMEM((208, 128), bf),
+            pltpu.VMEM((98, 128), f32), pltpu.VMEM((98, 128), f32),
+            pltpu.VMEM((2, 2, 8, 4, 8, 128), f32),
+            pltpu.VMEM((2, 4, 96, 128), f32), pltpu.VMEM((2, 8, 112, 128), f32),
+            pltpu.VMEM((2, 96, 128), f32), pltpu.VMEM((2, 112, 128), f32),
+            pltpu.VMEM((208, 128), f32),
+            dma((14,)), dma((14,)), dma((6,)), dma((6,)), dma((6,)), dma((6,)), dma((14,)), dma((14,)),
+            dma((2,)), dma((2,)), dma((13,)), dma((13,)),
+        ],
+        compiler_params=pltpu.CompilerParams(collective_id=1, has_side_effects=True, vmem_limit_bytes=60 * 1024 * 1024),
+        name="reduce_all",
+    )(s)
 
 
 def on_device(feature_map, proposals, hidden_weight, output_weight, upstream):
@@ -140,18 +332,39 @@
         "space",
     ).astype(jnp.float32)
     output_delta = gelu_grad(pre_output, upstream[0].astype(jnp.float32)).astype(jnp.bfloat16)
-    step_second = lax.dot_general(
-        hidden, output_delta, (((0,), (0,)), ((), ())), preferred_element_type=jnp.float32
-    )
-    second_total = lax.psum(step_second, "dp")
     hidden_back = lax.dot_general(
         output_delta, output_weight, (((1,), (1,)), ((), ())), preferred_element_type=jnp.float32
     )
     hidden_delta = gelu_grad(pre_hidden, hidden_back).astype(jnp.bfloat16)
-    step_first = lax.dot_general(
-        pooled, hidden_delta, (((0,), (0,)), ((), ())), preferred_element_type=jnp.float32
-    )
-    first_total = lax.psum_scatter(step_first, "dp", scatter_dimension=0, tiled=True)
+    core = lax.axis_index("dp") % 2
+
+    def half_of(array, which, width):
+        return lax.dynamic_slice_in_dim(array, which * width, width, 1)
+
+    def swapped(array):
+        return lax.ppermute(array, "dp", [(k, k ^ 1) for k in range(128)])
+
+    def both(left, right, width):
+        own = lax.dot_general(
+            left, half_of(right, core, width), (((0,), (0,)), ((), ())), preferred_element_type=jnp.float32
+        )
+        other = lax.dot_general(
+            swapped(left), swapped(half_of(right, 1 - core, width)), (((0,), (0,)), ((), ())),
+            preferred_element_type=jnp.float32,
+        )
+        return own + other
+
+    step_first = both(pooled, hidden_delta, 128)
+    step_second = both(hidden, output_delta, 256)
+    chunks = jnp.concatenate(
+        [
+            jnp.transpose(step_second.reshape(256, 2, 128), (1, 0, 2)).reshape(64, 8, 128),
+            step_first.reshape(64, 196, 128),
+            jnp.zeros((64, 4, 128), jnp.float32),
+        ],
+        axis=1,
+    )
+    first_total, second_total = reduce_all(chunks.reshape(2, 8, 4, 208, 128))
     partial_grad = lax.dot_general(
         hidden_delta, hidden_weight, (((1,), (1,)), ((), ())), preferred_element_type=jnp.float32
     )

time: 1240 us -> 293 us (0.24)
  waiting for transfers between devices: 685 us -> 21.8 us
  blocking collectives: 327 us -> 0 us
  Pallas kernels: 0 us -> 62.5 us
  between operations: 15.1 us -> 1 us
    psum x1 -> x0, waiting for transfers between devices: 669 us -> none  [on_device(): second_total = lax.psum(step_second, 'dp')]
    unnamed x1 -> x0, blocking collectives: 327 us -> none
    pallas_call x0 -> x1, Pallas kernels: none -> 62.5 us  [reduce_all(): pl.pallas_call(reduce_kernel, out_shape=(jax.ShapeDtypeStruct((98, 256),...]
    unnamed x8 -> x0, starting transfers between devices: 18.9 us -> none
  transfers between devices with their start and end apart: 12 -> 7, of which waited for: 4 -> 3; matrix products, arithmetic and copies ran while one was open for 27% -> 35% of each run, Pallas kernels for 0% -> 0%
where the time goes in v1:
time: 293 us; the launch traced here: 292 us
  matrix products  104 us (35%)
  local copies, waits for them, and re-layouts  73.8 us (25%)
  Pallas kernels  62.5 us (21%)
  waiting for transfers between devices  21.8 us (7%)
  starting transfers between devices  19.3 us (7%)
  other arithmetic  9.91 us (3%)
    pallas_call x1, Pallas kernels, reduce_all(): pl.pallas_call(reduce_kernel, out_shape=(jax.ShapeDtypeStruct((98, 256),...  62.5 us
    dot_general x4, matrix products, per_block(): jnp.einsum('riy,rjyc->rijc', row_part, across, precision=lax.Precision.HI...  29.9 us
    while x24, local copies, waits for them, and re-layouts  24.8 us
    dot_general x4, matrix products, per_block(): lax.dot_general(col_part.astype(jnp.float32).reshape(block_size * POOL, w...  23.4 us
    dot_general x4, matrix products, per_block(): jnp.einsum('riy,rijc->rjyc', row_part, grad_block, precision=lax.Precisio...  19.3 us
    all_to_all x2, waiting for transfers between devices, copy_for_each(): lax.all_to_all(jnp.broadcast_to(x[None], (size, *x.shape)), axis, 0, 0, t...  13.8 us
    convert_element_type x2, local copies, waits for them, and re-layouts, on_device(): pooled = crop_rows(whole_map, full_weight, col_weight).astype(jnp.bfloat16)  11.9 us
    dynamic_slice x4, local copies, waits for them, and re-layouts, crop_back(): total, _ = lax.scan(per_block, start, blocks)  10.8 us
  transfers between devices with their start and end apart: 7, of which 3 were waited for; matrix products, arithmetic and copies ran while one was open for 35% of the time, Pallas kernels for 0%

profile of v1, /device:TPU:1, one launch (start us, length us, event | category | flops | bytes accessed | tf_op | source)
XLA Modules:
  0.0 292.3 jit_solution(6993900471651755214)
XLA Ops:
  2.8 4.8 %all-to-all-start = ((bf16[2,12,84,256]{3,2,1,0:T(8,128)(2,1)}), bf16[2,12,84,256]{3,2,1,0:T(8,128)(2,1)S(1)}, u32[]{:S(2)}, u32[]{:S(2)}) async-start(bf16[2,12,84,256]{3,2,1,0:T(8,128)(2,1)} %broadcast_in_dim.20), calls=%async_computation | async-start | bytes 2162688 | tf_op jit(solution)/shard_map/all_to_all | solution.py:14
  9.5 11.8 %all-to-all-done = bf16[2,12,84,256]{3,2,1,0:T(8,128)(2,1)S(1)} async-done(((bf16[2,12,84,256]{3,2,1,0:T(8,128)(2,1)}), bf16[2,12,84,256]{3,2,1,0:T(8,128)(2,1)S(1)}, u32[]{:S(2)}, u32[]{:S(2)}) %all-to-all-start) | async-done | bytes 1032224 | tf_op jit(solution)/shard_map/all_to_all | solution.py:14
  21.8 34.6 %while.21 = (s32[]{:T(128)}, bf16[4,32,7,7,256]{4,2,3,1,0:T(8,128)(2,1)}, f32[4,32,7,24]{3,2,1,0:T(8,128)S(1)}, bf16[4,32,7,84]{3,1,0,2:T(8,128)(2,1)S(1)}, bf16[84,6144]{1,0:T(8,128)(2,1)S(1)}, /*index=5*/s32[]{:T(128)}) while((s32[]{:T(128)}, bf16[4,32,7,7,256]{4,2,3,1,0:T(8,128)(2,1)}, f32[4,32,7,24]{3,2,1,0:T(8,128)S(1)}, ...), condition=%wide.region_3.4_spmd, body=%wide.region_2.3_spmd.sunk | while | flops 346816512 | bytes 18293832 | solution.py:88
  23.0 7.4 %bitcast_dynamic-update-slice_fusion.2 = bf16[4,32,7,7,256]{4,2,3,1,0:T(8,128)(2,1)} fusion(bf16[4,32,7,7,256]{4,2,3,1,0:T(8,128)(2,1)} %get-tuple-element.203, s32[]{:T(128)} %get-tuple-element.202, f32[32,7,24,256]{3,0,2,1:T(8,128)S(1)} %fusion.72, f32[4,32,7,24]{3,2,1,0:T(8,128)S(1)} %get-tuple-element.210), kind=kOutput, calls=%fused_computation.2.clone.1 | convolution fusion | flops 115605504 | bytes 7472128 | tf_op jit(solution)/shard_map/while/body/eval_jaxpr/riy,rjyc->rijc/dot_general | solution.py:86
  31.6 7.5 %bitcast_dynamic-update-slice_fusion.2 = bf16[4,32,7,7,256]{4,2,3,1,0:T(8,128)(2,1)} fusion(bf16[4,32,7,7,256]{4,2,3,1,0:T(8,128)(2,1)} %get-tuple-element.203, s32[]{:T(128)} %get-tuple-element.202, f32[32,7,24,256]{3,0,2,1:T(8,128)S(1)} %fusion.72, f32[4,32,7,24]{3,2,1,0:T(8,128)S(1)} %get-tuple-element.210), kind=kOutput, calls=%fused_computation.2.clone.1 | convolution fusion | flops 115605504 | bytes 7472128 | tf_op jit(solution)/shard_map/while/body/eval_jaxpr/riy,rjyc->rijc/dot_general | solution.py:86
  40.3 7.5 %bitcast_dynamic-update-slice_fusion.2 = bf16[4,32,7,7,256]{4,2,3,1,0:T(8,128)(2,1)} fusion(bf16[4,32,7,7,256]{4,2,3,1,0:T(8,128)(2,1)} %get-tuple-element.203, s32[]{:T(128)} %get-tuple-element.202, f32[32,7,24,256]{3,0,2,1:T(8,128)S(1)} %fusion.72, f32[4,32,7,24]{3,2,1,0:T(8,128)S(1)} %get-tuple-element.210), kind=kOutput, calls=%fused_computation.2.clone.1 | convolution fusion | flops 115605504 | bytes 7472128 | tf_op jit(solution)/shard_map/while/body/eval_jaxpr/riy,rjyc->rijc/dot_general | solution.py:86
  48.9 7.5 %bitcast_dynamic-update-slice_fusion.2 = bf16[4,32,7,7,256]{4,2,3,1,0:T(8,128)(2,1)} fusion(bf16[4,32,7,7,256]{4,2,3,1,0:T(8,128)(2,1)} %get-tuple-element.203, s32[]{:T(128)} %get-tuple-element.202, f32[32,7,24,256]{3,0,2,1:T(8,128)S(1)} %fusion.72, f32[4,32,7,24]{3,2,1,0:T(8,128)S(1)} %get-tuple-element.210), kind=kOutput, calls=%fused_computation.2.clone.1 | convolution fusion | flops 115605504 | bytes 7472128 | tf_op jit(solution)/shard_map/while/body/eval_jaxpr/riy,rjyc->rijc/dot_general | solution.py:86
  56.4 5.2 %copy.41 = bf16[4,32,7,7,256]{4,3,2,1,0:T(8,128)(2,1)} copy(bf16[4,32,7,7,256]{4,2,3,1,0:T(8,128)(2,1)} %get-tuple-element.59) | data formatting | bytes 6422528 | tf_op jit(solution)/shard_map/convert_element_type | solution.py:327
  61.6 6.7 %convert_element_type.119 = bf16[128,12544]{1,0:T(8,128)(2,1)} reshape(bf16[4,32,7,7,256]{4,3,2,1,0:T(8,128)(2,1)} %copy.41) | data formatting | bytes 6422528 | tf_op jit(solution)/shard_map/convert_element_type | solution.py:327
  68.3 4.9 %multiply_convert_fusion.1 = (bf16[128,256]{1,0:T(8,128)(2,1)S(1)}, f32[128,256]{1,0:T(8,128)S(1)}) fusion(bf16[128,12544]{1,0:T(8,128)(2,1)} %convert_element_type.119, bf16[12544,256]{1,0:T(8,128)(2,1)} %param.13), kind=kOutput, calls=%fused_computation.54 | convolution fusion | flops 822378496 | bytes 9830400 | tf_op jit(solution)/shard_map/dot_general | solution.py:328
  84.0 4.0 %collective-permute-start.1 = (bf16[128,256]{1,0:T(8,128)(2,1)}, bf16[128,256]{1,0:T(8,128)(2,1)}, u32[]{:S(2)}, u32[]{:S(2)}) collective-permute-start(bf16[128,256]{1,0:T(8,128)(2,1)} %constant_dynamic-slice_fusion.3), channel_id=1, source_target_pairs={{0,2},{2,0},{4,6},{6,4},{8,10},{10,8},{12,14},{14,12},{16,18},{18,... | collective-permute-start | bytes 196616 | tf_op jit(solution)/shard_map/ppermute | solution.py:345
  88.2 7.8 %fusion.41 = f32[128,12544]{1,0:T(8,128)} fusion(bf16[128,256]{1,0:T(8,128)(2,1)S(1)} %fusion.34, bf16[12544,256]{1,0:T(8,128)(2,1)} %param.13), kind=kOutput, calls=%fused_computation.74 | convolution fusion | flops 822083584 | bytes 12910592 | tf_op jit(solution)/shard_map/dot_general | solution.py:368
  95.9 84.9 %while.22 = (s32[]{:T(128)}, f32[84,6144]{1,0:T(8,128)}, bf16[4,32,7,84]{3,2,1,0:T(8,128)(2,1)S(1)}, f32[4,32,12544]{2,1,0:T(8,128)}, f32[4,32,7,24]{3,2,1,0:T(8,128)S(1)}, /*index=5*/s32[]{:T(128)}, s32[]{:T(128)}) while((s32[]{:T(128)}, f32[84,6144]{1,0:T(8,128)}, bf16[4,32,7,84]{3,2,1,0:T(8,128)(2,1)S(1)}, ...), condition=%wide.region_6.7_spmd.clone, body=%wide.region_5.6_spmd.clone.sunk | while | flops 1503903744 | bytes 51240856 | solution.py:122
  100.4 4.8 %fusion.77 = f32[32,7,256,24]{2,3,1,0:T(8,128)S(1)} fusion(f32[32,7,7,256]{3,2,1,0:T(8,128)S(1)} %reshape.204, f32[4,32,7,24]{3,2,1,0:T(8,128)S(1)} %get-tuple-element.232, s32[]{:T(128)} %get-tuple-element.221), kind=kOutput, calls=%fused_computation.14.clone.1 | convolution fusion | flops 115605504 | bytes 7471108 | tf_op jit(solution)/shard_map/while/body/eval_jaxpr/riy,rijc->rjyc/dot_general | solution.py:106
  105.2 4.6 %copy.75 = f32[28,8,24,256]{3,1,2,0:T(8,128)} copy(f32[28,8,24,256]{3,2,1,0:T(8,128)S(1)} %bitcast.110) | data formatting | bytes 11010048 | tf_op jit(solution)/shard_map/while
  109.9 5.9 %convolution_add_fusion.4 = f32[84,6144]{1,0:T(8,128)S(1)} fusion(bf16[224,84]{1,0:T(8,128)(2,1)S(1)} %reshape.203, f32[224,6144]{1,0:T(8,128)} %bitcast.109, f32[84,6144]{1,0:T(8,128)S(1)} %copy-done.2, pred[]{:T(512)S(6)} %compare.4), kind=kOutput, calls=%fused_computation.13.clone.1 | convolution fusion | flops 1388298240 | bytes 9671425 | tf_op jit(solution)/shard_map/while/body/eval_jaxpr/dot_general | solution.py:107
  121.6 4.8 %fusion.77 = f32[32,7,256,24]{2,3,1,0:T(8,128)S(1)} fusion(f32[32,7,7,256]{3,2,1,0:T(8,128)S(1)} %reshape.204, f32[4,32,7,24]{3,2,1,0:T(8,128)S(1)} %get-tuple-element.232, s32[]{:T(128)} %get-tuple-element.221), kind=kOutput, calls=%fused_computation.14.clone.1 | convolution fusion | flops 115605504 | bytes 7471108 | tf_op jit(solution)/shard_map/while/body/eval_jaxpr/riy,rijc->rjyc/dot_general | solution.py:106
  126.5 4.6 %copy.75 = f32[28,8,24,256]{3,1,2,0:T(8,128)} copy(f32[28,8,24,256]{3,2,1,0:T(8,128)S(1)} %bitcast.110) | data formatting | bytes 11010048 | tf_op jit(solution)/shard_map/while
  131.1 5.9 %convolution_add_fusion.4 = f32[84,6144]{1,0:T(8,128)S(1)} fusion(bf16[224,84]{1,0:T(8,128)(2,1)S(1)} %reshape.203, f32[224,6144]{1,0:T(8,128)} %bitcast.109, f32[84,6144]{1,0:T(8,128)S(1)} %copy-done.2, pred[]{:T(512)S(6)} %compare.4), kind=kOutput, calls=%fused_computation.13.clone.1 | convolution fusion | flops 1388298240 | bytes 9671425 | tf_op jit(solution)/shard_map/while/body/eval_jaxpr/dot_general | solution.py:107
  142.8 4.8 %fusion.77 = f32[32,7,256,24]{2,3,1,0:T(8,128)S(1)} fusion(f32[32,7,7,256]{3,2,1,0:T(8,128)S(1)} %reshape.204, f32[4,32,7,24]{3,2,1,0:T(8,128)S(1)} %get-tuple-element.232, s32[]{:T(128)} %get-tuple-element.221), kind=kOutput, calls=%fused_computation.14.clone.1 | convolution fusion | flops 115605504 | bytes 7471108 | tf_op jit(solution)/shard_map/while/body/eval_jaxpr/riy,rijc->rjyc/dot_general | solution.py:106
  147.7 4.6 %copy.75 = f32[28,8,24,256]{3,1,2,0:T(8,128)} copy(f32[28,8,24,256]{3,2,1,0:T(8,128)S(1)} %bitcast.110) | data formatting | bytes 11010048 | tf_op jit(solution)/shard_map/while
  152.4 5.9 %convolution_add_fusion.4 = f32[84,6144]{1,0:T(8,128)S(1)} fusion(bf16[224,84]{1,0:T(8,128)(2,1)S(1)} %reshape.203, f32[224,6144]{1,0:T(8,128)} %bitcast.109, f32[84,6144]{1,0:T(8,128)S(1)} %copy-done.2, pred[]{:T(512)S(6)} %compare.4), kind=kOutput, calls=%fused_computation.13.clone.1 | convolution fusion | flops 1388298240 | bytes 9671425 | tf_op jit(solution)/shard_map/while/body/eval_jaxpr/dot_general | solution.py:107
  164.1 4.8 %fusion.77 = f32[32,7,256,24]{2,3,1,0:T(8,128)S(1)} fusion(f32[32,7,7,256]{3,2,1,0:T(8,128)S(1)} %reshape.204, f32[4,32,7,24]{3,2,1,0:T(8,128)S(1)} %get-tuple-element.232, s32[]{:T(128)} %get-tuple-element.221), kind=kOutput, calls=%fused_computation.14.clone.1 | convolution fusion | flops 115605504 | bytes 7471108 | tf_op jit(solution)/shard_map/while/body/eval_jaxpr/riy,rijc->rjyc/dot_general | solution.py:106
  168.9 4.6 %copy.75 = f32[28,8,24,256]{3,1,2,0:T(8,128)} copy(f32[28,8,24,256]{3,2,1,0:T(8,128)S(1)} %bitcast.110) | data formatting | bytes 11010048 | tf_op jit(solution)/shard_map/while
  173.6 5.9 %convolution_add_fusion.4 = f32[84,6144]{1,0:T(8,128)S(1)} fusion(bf16[224,84]{1,0:T(8,128)(2,1)S(1)} %reshape.203, f32[224,6144]{1,0:T(8,128)} %bitcast.109, f32[84,6144]{1,0:T(8,128)S(1)} %copy-done.2, pred[]{:T(512)S(6)} %compare.4), kind=kOutput, calls=%fused_computation.13.clone.1 | convolution fusion | flops 1388298240 | bytes 9671425 | tf_op jit(solution)/shard_map/while/body/eval_jaxpr/dot_general | solution.py:107
  184.0 3.8 %all-to-all-start.2 = ((bf16[2,12,84,256]{3,2,1,0:T(8,128)(2,1)}), bf16[2,12,84,256]{3,2,1,0:T(8,128)(2,1)S(1)}, u32[]{:S(2)}, u32[]{:S(2)}) async-start(bf16[2,12,84,256]{3,2,1,0:T(8,128)(2,1)} %bitcast.26), calls=%async_computation.2 | async-start | bytes 2162688 | tf_op jit(solution)/shard_map/all_to_all | solution.py:39
  187.9 5.7 %fusion.37 = f32[12544,128]{1,0:T(8,128)} fusion(bf16[128,12544]{1,0:T(8,128)(2,1)} %convert_element_type.119, bf16[128,256]{1,0:T(8,128)(2,1)S(1)} %fusion.34, s32[]{:T(128)S(6)} %select_n.22), kind=kOutput, calls=%fused_computation.58 | convolution fusion | flops 411041792 | bytes 9666564 | tf_op jit(solution)/shard_map/dot_general | solution.py:348
  195.2 8.0 %all-to-all-done.2 = bf16[2,12,84,256]{3,2,1,0:T(8,128)(2,1)S(1)} async-done(((bf16[2,12,84,256]{3,2,1,0:T(8,128)(2,1)}), bf16[2,12,84,256]{3,2,1,0:T(8,128)(2,1)S(1)}, u32[]{:S(2)}, u32[]{:S(2)}) %all-to-all-start.2) | async-done | bytes 1032224 | tf_op jit(solution)/shard_map/all_to_all | solution.py:39
  205.0 7.5 %convolution_add_fusion.1 = f32[12544,128]{1,0:T(8,128)} fusion(f32[12544,128]{1,0:T(8,128)} %fusion.37, bf16[128,12544]{1,0:T(8,128)(2,1)} %collective-permute-done.2, bf16[128,128]{1,0:T(8,128)(2,1)S(1)} %collective-permute-done.3), kind=kOutput, calls=%fused_computation.21 | convolution fusion | flops 412647424 | bytes 16089088 | tf_op jit(solution)/shard_map/dot_general | solution.py:351
  212.6 7.3 %concatenate.9 = f32[2,8,4,196,128]{4,3,2,1,0:T(8,128)} reshape(f32[12544,128]{1,0:T(8,128)} %convolution_add_fusion.1) | data formatting | bytes 12845056 | tf_op jit(solution)/shard_map/concatenate | solution.py:359
  219.9 6.5 %maximum_maximum_fusion.s_ref = f32[2,8,4,208,128]{4,3,2,1,0:T(8,128)} fusion(f32[2,8,4,196,128]{4,3,2,1,0:T(8,128)} %concatenate.9, f32[2,8,4,8,128]{4,3,2,1,0:T(8,128)S(1)} %bitcast.122, f32[208]{0:T(256)S(1)} %pad.2.clone), kind=kLoop, calls=%fused_computation.22 | loop fusion | flops 3407872 | bytes 13501248 | tf_op jit(solution)/shard_map/concatenate | solution.py:359
  226.3 62.5 %reduce_all.1 = (f32[98,256]{1,0:T(8,128)}, f32[256,512]{1,0:T(8,128)}) custom-call(f32[2,8,4,208,128]{4,3,2,1,0:T(8,128)} %maximum_maximum_fusion.s_ref), custom_call_target="tpu_custom_call" | custom-call | tf_op jit(solution)/shard_map/reduce_all/pallas_call | solution.py:291
  (103 shorter events, 53.5 us)
Async XLA Ops:
  0.6 72.6 %copy-start = (bf16[256,512]{1,0:T(8,128)(2,1)S(1)}, bf16[256,512]{1,0:T(8,128)(2,1)}, u32[]{:S(2)}) copy-start(bf16[256,512]{1,0:T(8,128)(2,1)} %param.14) | copy-start | bytes 786436
  0.6 7.1 %copy-start.6 = (f32[2]{0:T(128)S(1)}, f32[2]{0:T(128)}, u32[]{:S(2)}) copy-start(f32[2]{0:T(128)} %constant.88.clone) | copy-start | bytes 28
  0.7 7.0 %copy-start.5 = (s32[1,128,4]{1,2,0:T(4,128)S(1)}, s32[1,128,4]{1,2,0:T(4,128)}, u32[]{:S(2)}) copy-start(s32[1,128,4]{1,2,0:T(4,128)} %param.12) | copy-start | bytes 6148
  2.8 18.4 %all-to-all-start = ((bf16[2,12,84,256]{3,2,1,0:T(8,128)(2,1)}), bf16[2,12,84,256]{3,2,1,0:T(8,128)(2,1)S(1)}, u32[]{:S(2)}, u32[]{:S(2)}) async-start(bf16[2,12,84,256]{3,2,1,0:T(8,128)(2,1)} %broadcast_in_dim.20), calls=%async_computation | async-start | bytes 2162688 | tf_op jit(solution)/shard_map/all_to_all | solution.py:14
  68.3 14.8 %copy-start.4 = (bf16[1,128,512]{2,1,0:T(8,128)(2,1)S(1)}, bf16[1,128,512]{2,1,0:T(8,128)(2,1)}, u32[]{:S(2)}) copy-start(bf16[1,128,512]{2,1,0:T(8,128)(2,1)} %param.15) | copy-start | bytes 393220
  74.1 9.0 %all-to-all-start.1 = ((bf16[2,128,512]{2,1,0:T(8,128)(2,1)}), bf16[2,128,512]{2,1,0:T(8,128)(2,1)S(1)}, u32[]{:S(2)}, u32[]{:S(2)}) async-start(bf16[2,128,512]{2,1,0:T(8,128)(2,1)} %broadcast_in_dim.21), calls=%async_computation.1 | async-start | bytes 524288 | tf_op jit(solution)/shard_map/all_to_all | solution.py:14
  77.9 116.0 %collective-permute-start = (bf16[128,256]{1,0:T(8,128)(2,1)S(1)}, bf16[128,256]{1,0:T(8,128)(2,1)}, u32[]{:S(2)}, u32[]{:S(2)}) collective-permute-start(bf16[128,256]{1,0:T(8,128)(2,1)S(1)} %get-tuple-element.132), channel_id=1, source_target_pairs={{0,2},{2,0},{4,6},{6,4},{8,10},{10,8},{12,14},{14,12},{16,18},{18,... | collective-permute-start | bytes 196616 | tf_op jit(solution)/shard_map/ppermute | solution.py:345
  80.9 124.1 %collective-permute-start.2 = (bf16[128,12544]{1,0:T(8,128)(2,1)}, bf16[128,12544]{1,0:T(8,128)(2,1)}, u32[]{:S(2)}, u32[]{:S(2)}) collective-permute-start(bf16[128,12544]{1,0:T(8,128)(2,1)} %convert_element_type.119), channel_id=1, source_target_pairs={{0,2},{2,0},{4,6},{6,4},{8,10},{10,8},{12,14},{14,12},{16,18},{18,... | collective-permute-start | bytes 9633800 | tf_op jit(solution)/shard_map/ppermute | solution.py:345
  84.0 110.0 %collective-permute-start.1 = (bf16[128,256]{1,0:T(8,128)(2,1)}, bf16[128,256]{1,0:T(8,128)(2,1)}, u32[]{:S(2)}, u32[]{:S(2)}) collective-permute-start(bf16[128,256]{1,0:T(8,128)(2,1)} %constant_dynamic-slice_fusion.3), channel_id=1, source_target_pairs={{0,2},{2,0},{4,6},{6,4},{8,10},{10,8},{12,14},{14,12},{16,18},{18,... | collective-permute-start | bytes 196616 | tf_op jit(solution)/shard_map/ppermute | solution.py:345
  105.2 4.7 %copy-start.2 = (f32[84,6144]{1,0:T(8,128)S(1)}, f32[84,6144]{1,0:T(8,128)}, u32[]{:S(2)}) copy-start(f32[84,6144]{1,0:T(8,128)} %get-tuple-element.222) | copy-start | bytes 6193156 | tf_op jit(solution)/shard_map/while
  115.8 1.3 copy-start.3
  126.5 4.7 %copy-start.2 = (f32[84,6144]{1,0:T(8,128)S(1)}, f32[84,6144]{1,0:T(8,128)}, u32[]{:S(2)}) copy-start(f32[84,6144]{1,0:T(8,128)} %get-tuple-element.222) | copy-start | bytes 6193156 | tf_op jit(solution)/shard_map/while
  137.0 1.3 copy-start.3
  147.7 4.7 %copy-start.2 = (f32[84,6144]{1,0:T(8,128)S(1)}, f32[84,6144]{1,0:T(8,128)}, u32[]{:S(2)}) copy-start(f32[84,6144]{1,0:T(8,128)} %get-tuple-element.222) | copy-start | bytes 6193156 | tf_op jit(solution)/shard_map/while
  158.2 1.3 copy-start.3
  168.9 4.7 %copy-start.2 = (f32[84,6144]{1,0:T(8,128)S(1)}, f32[84,6144]{1,0:T(8,128)}, u32[]{:S(2)}) copy-start(f32[84,6144]{1,0:T(8,128)} %get-tuple-element.222) | copy-start | bytes 6193156 | tf_op jit(solution)/shard_map/while
  179.5 1.3 copy-start.3
  184.0 19.1 %all-to-all-start.2 = ((bf16[2,12,84,256]{3,2,1,0:T(8,128)(2,1)}), bf16[2,12,84,256]{3,2,1,0:T(8,128)(2,1)S(1)}, u32[]{:S(2)}, u32[]{:S(2)}) async-start(bf16[2,12,84,256]{3,2,1,0:T(8,128)(2,1)} %bitcast.26), calls=%async_computation.2 | async-start | bytes 2162688 | tf_op jit(solution)/shard_map/all_to_all | solution.py:39
  193.8 11.2 %collective-permute-start.3 = (bf16[128,128]{1,0:T(8,128)(2,1)S(1)}, bf16[128,128]{1,0:T(8,128)(2,1)S(1)}, u32[]{:S(2)}, u32[]{:S(2)}) collective-permute-start(bf16[128,128]{1,0:T(8,128)(2,1)S(1)} %constant_dynamic-slice_fusion.2), channel_id=1, source_target_pairs={{0,2},{2,0},{4,6},{6,4},{8,10},{10,8},{12,14},{14,12},{16,18},{18,... | collective-permute-start | bytes 98312 | tf_op jit(solution)/shard_map/ppermute | solution.py:345
  219.9 72.4 %copy-start.1 = (bf16[256,512]{1,0:T(8,128)(2,1)S(1)}, bf16[256,512]{1,0:T(8,128)(2,1)}, u32[]{:S(2)}) copy-start(bf16[256,512]{1,0:T(8,128)(2,1)} %param.14) | copy-start | bytes 786436

commit v2 on v1

v2 whole, which is shorter than its diff:
```python
import jax
import jax.numpy as jnp
from jax import lax
from jax.experimental import pallas as pl
from jax.experimental.pallas import tpu as pltpu
from jax.sharding import PartitionSpec as P

MESH = pl.DeviceIdType.MESH
POOL = 7
ROIS = 128
CHANNELS = 256
ROWS = 12
COLS = 84
PITCH = 96
HALF = ROWS * PITCH
BINS = POOL * ROIS
WIDE = POOL * CHANNELS
BF = jnp.bfloat16
F32 = jnp.float32
TN = (((0,), (0,)), ((), ()))
NT = (((1,), (1,)), ((), ()))
SCALE = 0.7978845608028654
CUBIC = 0.044715


def gelu_of(v):
    return 0.5 * v * (1.0 + jnp.tanh(SCALE * (v + CUBIC * v * v * v)))


def gelu_slope(v):
    t = jnp.tanh(SCALE * (v + CUBIC * v * v * v))
    return 0.5 * (1.0 + t) + 0.5 * v * (1.0 - t * t) * (SCALE * (1.0 + 3.0 * CUBIC * v * v))


def place():
    me = lax.axis_index("dp")
    return me // 64, (me // 8) % 8, (me // 2) % 4, me % 2


def index_of(x, z, y, c):
    return ((x * 8 + z) * 4 + y) * 2 + c


def chains_of(hops):
    return ((0, 1, hops), (1, -1, hops), (0, -1, hops - 1), (1, 1, hops - 1))


def step_kernel(
    fm_ref, corner_ref, hw_hbm, ow_ref, up_ref, first_ref, second_ref, map_ref,
    hw_ref, feat, far, row_all, col_all, weights, pooled, hid_acc,
    z_s, z_r, hd_own, hd_pair, hd_s, od_pair, od_s, hid_pair, s_flat, chunks, grads, map_acc, map_s, map_r,
    za_s, za_r, yb_s, yb_r, ya_s, ya_r, zb_s, zb_r, x_s, x_r, c_s, c_r, gather,
    acc_a, acc_b, mid_a, mid_b, final,
    hw_sem, f_sem, p_ss, p_rs, m_ss, m_rs,
    za_ss, za_rs, yb_ss, yb_rs, ya_ss, ya_rs, zb_ss, zb_rs, xc_ss, xc_rs, g_ss, g_rs,
):
    x, z, y, c = place()
    s = lax.axis_index("space")

    def at_z(step):
        return {"dp": index_of(x, (z + step + 8) % 8, y, c)}

    def at_y(step):
        return {"dp": index_of(x, z, (y + step + 4) % 4, c)}

    at_x = {"dp": index_of(1 - x, z, y, c)}
    at_c = {"dp": index_of(x, z, y, 1 - c)}
    at_s = {"space": 1 - s}

    load_hw = pltpu.make_async_copy(hw_hbm, hw_ref, hw_sem)
    load_hw.start()
    barrier = pltpu.get_barrier_semaphore()
    peers = [at_s, at_c] + [at_z(k) for k in range(1, 8)] + [at_y(k) for k in range(1, 4)] + [at_x]
    for peer in peers:
        pl.semaphore_signal(barrier, inc=1, device_id=peer, device_id_type=MESH)
    pl.semaphore_wait(barrier, len(peers))

    copies = []

    def one(src, dst, ssem, rsem, peer):
        copy = pltpu.make_async_remote_copy(
            src_ref=src, dst_ref=dst, send_sem=ssem, recv_sem=rsem, device_id=peer, device_id_type=MESH
        )
        copy.start()
        copies.append(copy)
        return copy

    features = one(fm_ref, far, f_sem.at[0], f_sem.at[1], at_s)

    feat[...] = jnp.zeros((2 * HALF, CHANNELS), BF)
    for row in range(ROWS):
        feat[row * PITCH:row * PITCH + COLS] = fm_ref[row]
    lane = lax.broadcasted_iota(jnp.int32, (ROIS, 128), 1).astype(F32)
    base = (ROWS * s).astype(F32)
    row_at = jnp.where(lane < ROWS, lane + base, lane - base)
    spot = lax.broadcasted_iota(jnp.int32, (128, 2 * HALF), 1).astype(F32)
    slot_at = lax.broadcasted_iota(jnp.int32, (128, 2 * HALF), 0).astype(F32)
    row_of = jnp.floor((spot + 0.5) * (1.0 / PITCH))
    row_pick = (row_of == slot_at).astype(F32).astype(BF)
    col_pick = jnp.logical_and(spot - row_of * PITCH == slot_at, slot_at < COLS).astype(F32).astype(BF)

    def bins(low, high, grid, k):
        start = corner_ref[:, low:low + 1].astype(F32)
        size = (corner_ref[:, high:high + 1] - corner_ref[:, low:low + 1]).astype(F32) / POOL
        total = jnp.zeros((ROIS, 128), F32)
        for offset in (0.25, 0.75):
            point = start + (k + offset) * size - 0.5
            total = total + jnp.maximum(0.0, 1.0 - jnp.abs(point - grid))
        return (0.5 * total).astype(BF)

    for k in range(POOL):
        row_all[k] = jnp.dot(bins(0, 2, row_at, k), row_pick, preferred_element_type=F32).astype(BF)
        col_all[k] = jnp.dot(bins(1, 3, lane, k), col_pick, preferred_element_type=F32).astype(BF)

    def build(i, half):
        at = half * HALF
        for j in range(POOL):
            weights[j * ROIS:(j + 1) * ROIS, at:at + HALF] = col_all[j, :, at:at + HALF] * row_all[i, :, at:at + HALF]
        return weights[:, at:at + HALF]

    def near_part(i, _):
        value = jnp.dot(build(i, 0), feat[0:HALF], preferred_element_type=F32)
        for k in range(2):
            s_flat[pl.ds(pl.multiple_of((k * POOL + i) * BINS, BINS), BINS)] = value[:, k * 128:(k + 1) * 128]
        return 0

    lax.fori_loop(0, POOL, near_part, 0)
    features.wait_recv()
    for row in range(ROWS):
        at = HALF + row * PITCH
        feat[at:at + COLS] = far[row]
    load_hw.wait()
    hid_acc[...] = jnp.zeros((ROIS, CHANNELS), F32)

    def share(i):
        return pltpu.make_async_remote_copy(
            src_ref=pooled.at[i, 0:ROIS], dst_ref=pooled.at[i, ROIS:2 * ROIS],
            send_sem=p_ss.at[i], recv_sem=p_rs.at[i], device_id=at_c, device_id_type=MESH,
        )

    def far_part(i, _):
        value = jnp.dot(build(i, 1), feat[HALF:2 * HALF], preferred_element_type=F32)
        near = [s_flat[pl.ds(pl.multiple_of((k * POOL + i) * BINS, BINS), BINS)] for k in range(2)]
        value = (value + jnp.concatenate(near, axis=1)).astype(BF)
        for j in range(POOL):
            pooled[i, 0:ROIS, j * CHANNELS:(j + 1) * CHANNELS] = value[j * ROIS:(j + 1) * ROIS]
        share(i).start()
        hid_acc[...] += jnp.dot(
            pooled[i, 0:ROIS], hw_ref[pl.ds(pl.multiple_of(i * WIDE, WIDE), WIDE)], preferred_element_type=F32
        )
        return 0

    lax.fori_loop(0, POOL, far_part, 0)

    pre_hidden = hid_acc[...]
    hidden = gelu_of(pre_hidden).astype(BF)
    part = jnp.dot(hidden, ow_ref[...], preferred_element_type=F32)
    z_s[...] = part.astype(BF)
    swap_z = one(z_s, z_r, m_ss.at[0], m_rs.at[0], at_s)
    hid_pair[0:ROIS] = hidden
    send_hid = one(hid_pair.at[0:ROIS], hid_pair.at[ROIS:2 * ROIS], m_ss.at[1], m_rs.at[1], at_c)
    slope = gelu_slope(pre_hidden)
    swap_z.wait_recv()
    pre_output = part + z_r[...].astype(F32)
    delta = (up_ref[...].astype(F32) * gelu_slope(pre_output)).astype(BF)
    od_pair[0:ROIS] = jnp.where(c == 0, delta[:, 0:256], delta[:, 256:512])
    od_s[...] = jnp.where(c == 0, delta[:, 256:512], delta[:, 0:256])
    send_od = one(od_s, od_pair.at[ROIS:2 * ROIS], m_ss.at[2], m_rs.at[2], at_c)
    back = lax.dot_general(delta, ow_ref[...], NT, preferred_element_type=F32)
    hidden_delta = (back * slope).astype(BF)
    hd_own[...] = hidden_delta
    hd_pair[0:ROIS] = jnp.where(c == 0, hidden_delta[:, 0:128], hidden_delta[:, 128:256])
    hd_s[...] = jnp.where(c == 0, hidden_delta[:, 128:256], hidden_delta[:, 0:128])
    send_hd = one(hd_s, hd_pair.at[ROIS:2 * ROIS], m_ss.at[3], m_rs.at[3], at_c)

    def wait_share(i, _):
        share(i).wait_recv()
        return 0

    send_hid.wait_recv()
    send_od.wait_recv()
    second = lax.dot_general(hid_pair[...], od_pair[...], TN, preferred_element_type=F32)
    for u in range(2):
        chunks[u, :, :, 0:8, :] = second[:, u * 128:(u + 1) * 128].reshape(8, 4, 8, 128)
        chunks[u, :, :, 200:208, :] = jnp.zeros((8, 4, 8, 128), F32)
    lax.fori_loop(0, POOL, wait_share, 0)
    send_hd.wait_recv()

    def weight_part(i, _):
        s_flat[pl.ds(pl.multiple_of(i * WIDE, WIDE), WIDE)] = lax.dot_general(
            pooled[i], hd_pair[...], TN, preferred_element_type=F32
        )
        return 0

    lax.fori_loop(0, POOL, weight_part, 0)

    def regroup(k, _):
        chunks[k // 32, (k // 4) % 8, k % 4, 8:204, :] = s_flat[pl.ds(k * 196, 196)]
        return 0

    lax.fori_loop(0, 64, regroup, 0)

    def ring(size, pos, to, own, send, recv, ssem, rsem):
        chains = chains_of(size // 2)
        live = {}

        def slot(k, h):
            return sum(ch[2] for ch in chains[:k]) + h

        def go(k, h):
            u, way, hops = chains[k]
            if h > 0:
                live[k, h - 1].wait_recv()
            dest = (pos + way * (hops - h) + size) % size
            value = own(u, dest)
            if h > 0:
                value = value + recv[slot(k, h - 1)].astype(F32)
            at = slot(k, h)
            send[at] = value.astype(BF)
            live[k, h] = pltpu.make_async_remote_copy(
                src_ref=send.at[at], dst_ref=recv.at[at], send_sem=ssem.at[at], recv_sem=rsem.at[at],
                device_id=to(way), device_id_type=MESH,
            )
            live[k, h].start()
            copies.append(live[k, h])

        def total(u):
            value = own(u, pos)
            for k, (piece, _, hops) in enumerate(chains):
                if piece == u and hops > 0:
                    live[k, hops - 1].wait_recv()
                    value = value + recv[slot(k, hops - 1)].astype(F32)
            return value

        return go, total

    za_go, za_total = ring(8, z, at_z, lambda u, d: chunks[u, d, :, 0:96, :], za_s, za_r, za_ss, za_rs)
    yb_go, yb_total = ring(4, y, at_y, lambda u, d: chunks[u, :, d, 96:208, :], yb_s, yb_r, yb_ss, yb_rs)
    ya_go, ya_total = ring(4, y, at_y, lambda u, d: acc_a[u, d], ya_s, ya_r, ya_ss, ya_rs)
    zb_go, zb_total = ring(8, z, at_z, lambda u, d: acc_b[u, d], zb_s, zb_r, zb_ss, zb_rs)

    def back_part(half):
        at = half * HALF

        def body(i, _):
            if half == 1:
                g = lax.dot_general(
                    hw_ref[pl.ds(pl.multiple_of(i * WIDE, WIDE), WIDE)], hd_own[...], NT, preferred_element_type=F32
                ).astype(BF)
                for j in range(POOL):
                    grads[i, :, j * ROIS:(j + 1) * ROIS] = g[j * CHANNELS:(j + 1) * CHANNELS]
            map_acc[:, at:at + HALF] += jnp.dot(grads[i], build(i, half), preferred_element_type=F32)
            return 0

        return body

    def work(half, low, high):
        lax.fori_loop(low, high, back_part(half), 0)

    for k in (0, 1):
        za_go(k, 0)
    for k in (0, 1):
        yb_go(k, 0)
    for k in (2, 3):
        za_go(k, 0)
    for k in (2, 3):
        yb_go(k, 0)
    map_acc[...] = jnp.zeros((CHANNELS, 2 * HALF), F32)
    work(1, 0, 3)
    for k in (0, 1, 2, 3):
        za_go(k, 1)
    for k in (0, 1):
        yb_go(k, 1)
    work(1, 3, 7)
    map_s[...] = jnp.transpose(map_acc[:, HALF:2 * HALF]).astype(BF)
    swap_map = one(map_s, map_r, m_ss.at[4], m_rs.at[4], at_s)
    for k in (0, 1, 2, 3):
        za_go(k, 2)
    work(0, 0, 3)
    for k in (0, 1):
        za_go(k, 3)
    for u in (0, 1):
        acc_b[u] = yb_total(u)
        zb_go(u, 0)
    for k in (2, 3):
        zb_go(k, 0)
    work(0, 3, 7)
    for u in (0, 1):
        acc_a[u] = za_total(u)
        ya_go(u, 0)
    for k in (2, 3):
        ya_go(k, 0)
    for k in (0, 1, 2, 3):
        zb_go(k, 1)
    for k in (0, 1):
        ya_go(k, 1)
    for k in (0, 1, 2, 3):
        zb_go(k, 2)
    near = jnp.transpose(map_acc[:, 0:HALF])
    for u in (0, 1):
        mid_a[u] = ya_total(u)
    for k in (0, 1):
        zb_go(k, 3)
    swap_map.wait_recv()
    whole = near + map_r[...].astype(F32)
    for row in range(ROWS):
        map_ref[row] = whole[row * PITCH:row * PITCH + COLS]
    for u in (0, 1):
        mid_b[u] = zb_total(u)

    x_s[0:96] = mid_a[1 - x].astype(BF)
    x_s[96:208] = mid_b[1 - x].astype(BF)
    across = one(x_s, x_r, xc_ss.at[0], xc_rs.at[0], at_x)
    across.wait_recv()
    final[0:96] = mid_a[x] + x_r[0:96].astype(F32)
    final[96:208] = mid_b[x] + x_r[96:208].astype(F32)

    gather[c, x, z, y] = final[0:8]
    mine = gather.at[c, x, z, y]
    steps = [one(mine, mine, g_ss.at[k], g_rs.at[k], at_z(k)) for k in range(1, 8)]
    low, high = final[8:106], final[106:204]
    c_s[...] = jnp.where(c == 0, high, low)
    swap = one(c_s, c_r, xc_ss.at[1], xc_rs.at[1], at_c)
    swap.wait_recv()
    kept = jnp.where(c == 0, low, high)
    got = c_r[...]
    first_ref[:, 0:128] = jnp.where(c == 0, kept, got)
    first_ref[:, 128:256] = jnp.where(c == 0, got, kept)
    for step in steps:
        step.wait_recv()
    steps = []
    for k in range(1, 4):
        column = gather.at[c, x, :, y]
        steps.append(one(column, column, g_ss.at[7 + k], g_rs.at[7 + k], at_y(k)))
    for step in steps:
        step.wait_recv()
    plane = gather.at[c, x]
    one(plane, plane, g_ss.at[11], g_rs.at[11], at_x).wait_recv()
    half = gather.at[c]
    one(half, half, g_ss.at[12], g_rs.at[12], at_c).wait_recv()
    for k in range(2):
        for u in range(2):
            at = k * 256 + u * 128
            second_ref[:, at:at + 128] = gather[k, u].reshape(256, 128)
    for copy in copies:
        copy.wait_send()

    def sent(i, _):
        share(i).wait_send()
        return 0

    lax.fori_loop(0, POOL, sent, 0)


def on_device(feature_map, proposals, hidden_weight, output_weight, upstream):
    dma = pltpu.SemaphoreType.DMA
    vmem = pl.BlockSpec(memory_space=pltpu.VMEM)
    first, second, grad = pl.pallas_call(
        step_kernel,
        out_shape=(
            jax.ShapeDtypeStruct((98, 256), F32),
            jax.ShapeDtypeStruct((256, 512), F32),
            jax.ShapeDtypeStruct((ROWS, COLS, CHANNELS), F32),
        ),
        in_specs=[vmem, vmem, pl.BlockSpec(memory_space=pl.ANY), vmem, vmem],
        out_specs=[vmem] * 3,
        scratch_shapes=[
            pltpu.VMEM((POOL * WIDE, 256), BF),
            pltpu.VMEM((2 * HALF, CHANNELS), BF),
            pltpu.VMEM((ROWS, COLS, CHANNELS), BF),
            pltpu.VMEM((POOL, ROIS, 2 * HALF), BF),
            pltpu.VMEM((POOL, ROIS, 2 * HALF), BF),
            pltpu.VMEM((BINS, 2 * HALF), BF),
            pltpu.VMEM((POOL, 2 * ROIS, WIDE), BF),
            pltpu.VMEM((ROIS, CHANNELS), F32),
            pltpu.VMEM((ROIS, 512), BF), pltpu.VMEM((ROIS, 512), BF),
            pltpu.VMEM((ROIS, 256), BF),
            pltpu.VMEM((2 * ROIS, 128), BF), pltpu.VMEM((ROIS, 128), BF),
            pltpu.VMEM((2 * ROIS, 256), BF), pltpu.VMEM((ROIS, 256), BF),
            pltpu.VMEM((2 * ROIS, 256), BF),
            pltpu.VMEM((POOL * WIDE, 128), F32),
            pltpu.VMEM((2, 8, 4, 208, 128), F32),
            pltpu.VMEM((POOL, CHANNELS, BINS), BF),
            pltpu.VMEM((CHANNELS, 2 * HALF), F32),
            pltpu.VMEM((HALF, CHANNELS), BF), pltpu.VMEM((HALF, CHANNELS), BF),
            pltpu.VMEM((14, 4, 96, 128), BF), pltpu.VMEM((14, 4, 96, 128), BF),
            pltpu.VMEM((6, 8, 112, 128), BF), pltpu.VMEM((6, 8, 112, 128), BF),
            pltpu.VMEM((6, 96, 128), BF), pltpu.VMEM((6, 96, 128), BF),
            pltpu.VMEM((14, 112, 128), BF), pltpu.VMEM((14, 112, 128), BF),
            pltpu.VMEM((208, 128), BF), pltpu.VMEM((208, 128), BF),
            pltpu.VMEM((98, 128), F32), pltpu.VMEM((98, 128), F32),
            pltpu.VMEM((2, 2, 8, 4, 8, 128), F32),
            pltpu.VMEM((2, 4, 96, 128), F32), pltpu.VMEM((2, 8, 112, 128), F32),
            pltpu.VMEM((2, 96, 128), F32), pltpu.VMEM((2, 112, 128), F32),
            pltpu.VMEM((208, 128), F32),
            dma(()), dma((2,)), dma((POOL,)), dma((POOL,)), dma((5,)), dma((5,)),
            dma((14,)), dma((14,)), dma((6,)), dma((6,)), dma((6,)), dma((6,)), dma((14,)), dma((14,)),
            dma((2,)), dma((2,)), dma((13,)), dma((13,)),
        ],
        compiler_params=pltpu.CompilerParams(
            collective_id=1, has_side_effects=True, vmem_limit_bytes=67043328
        ),
        name="box_head_step",
    )(feature_map[0], proposals[0], hidden_weight, output_weight, upstream[0])
    return (first, second, grad[None])


def solution(mesh):
    placed = (
        P("dp", "space", None, None),
        P("dp", None, None),
        P(None, "space"),
        P("space", None),
        P("dp", None, None),
    )
    return jax.shard_map(
        on_device,
        mesh=mesh,
        in_specs=placed,
        out_specs=(P("dp", "space"), P("space", None), P("dp", "space", None, None)),
        check_vma=False,
    )
```

time: 293 us -> 107 us (0.37)
  matrix products: 104 us -> 0 us
  local copies, waits for them, and re-layouts: 73.8 us -> 8.09 us
  Pallas kernels: 62.5 us -> 98.5 us
  waiting for transfers between devices: 21.8 us -> 0 us
  starting transfers between devices: 19.3 us -> 0 us
  other arithmetic: 9.91 us -> 0 us
    dot_general x24 -> x0, matrix products: 104 us -> none  [the longest x4 29.9 us: per_block(): jnp.einsum('riy,rjyc->rijc', row_part, across, precision=lax.Precision.HI...]
    pallas_call x1, Pallas kernels: 62.5 us -> 98.5 us  [on_device(): pl.pallas_call(step_kernel, out_shape=(jax.ShapeDtypeStruct((98, 256), F3...]
    while x25 -> x0, local copies, waits for them, and re-layouts: 25 us -> none
    all_to_all x3 -> x0, waiting for transfers between devices: 21.8 us -> none  [the longest x2 13.8 us: copy_for_each(): lax.all_to_all(jnp.broadcast_to(x[None], (size, *x.shape)), axis, 0, 0, t...]
    convert_element_type x6 -> x0, local copies, waits for them, and re-layouts: 13.6 us -> none  [the longest x2 11.9 us: on_device(): pooled = crop_rows(whole_map, full_weight, col_weight).astype(jnp.bfloat16)]
    all_to_all x3 -> x0, starting transfers between devices: 12.1 us -> none  [the longest x2 8.27 us: copy_for_each(): lax.all_to_all(jnp.broadcast_to(x[None], (size, *x.shape)), axis, 0, 0, t...]
    dynamic_slice x10 -> x0, local copies, waits for them, and re-layouts: 11.5 us -> none  [the longest x4 10.8 us: crop_back(): total, _ = lax.scan(per_block, start, blocks)]
    reshape x9 -> x0, local copies, waits for them, and re-layouts: 7.38 us -> none  [the longest x4 7.12 us: per_block(): grad_block = grad_part.reshape(block_size, POOL, POOL, channels)]
  transfers between devices with their start and end apart: 7 -> 0, of which waited for: 3 -> 0; matrix products, arithmetic and copies ran while one was open for 35% -> 0% of each run, Pallas kernels for 0% -> 0%
where the time goes in v2:
time: 107 us
  Pallas kernels  98.5 us (92%)
  local copies, waits for them, and re-layouts  8.09 us (8%)
    pallas_call x1, Pallas kernels, on_device(): pl.pallas_call(step_kernel, out_shape=(jax.ShapeDtypeStruct((98, 256), F3...  98.5 us
    unnamed x4, local copies, waits for them, and re-layouts  8.09 us

profile of v2, /device:TPU:1, one launch (start us, length us, event | category | flops | bytes accessed | tf_op | source)
XLA Modules:
  0.0 107.2 jit_solution(1393455104509268340)
XLA Ops:
  0.6 1.4 %copy.8 = s32[1,128,4]{2,1,0:T(8,128)} copy(s32[1,128,4]{1,2,0:T(4,128)} %param.6) | data formatting | bytes 4096 | tf_op args[1]
  2.0 98.5 %box_head_step.1 = (f32[98,256]{1,0:T(8,128)}, f32[256,512]{1,0:T(8,128)}, f32[12,84,256]{2,1,0:T(8,128)}) custom-call(bf16[12,84,256]{2,1,0:T(8,128)(2,1)} %bitcast.5, s32[128,4]{1,0:T(8,128)} %bitcast.6, bf16[12544,256]{1,0:T(8,128)(2,1)} %hw_hbm.1, bf16[256,512]{1,0:T(8,128)(2,1)} %ow_ref.1, bf16[128,512]{1,0:T(8,128)(2,1)} %bitcast.7), custom_call_target="tpu_custom_call" | custom-call | tf_op jit(solution)/shard_map/box_head_step/pallas_call | solution.py:358
  100.6 3.3 %copy.9 = f32[1,12,84,256]{3,0,2,1:T(1,128)} copy(f32[1,12,84,256]{3,2,1,0:T(8,128)} %bitcast.4) | data formatting | bytes 2064384
  103.8 1.5 %copy.12 = f32[98,256]{1,0:T(8,128)} copy(f32[98,256]{1,0:T(8,128)} %get-tuple-element.15) | data formatting | bytes 200704
  105.4 1.9 %copy.13 = f32[256,512]{1,0:T(8,128)} copy(f32[256,512]{1,0:T(8,128)} %get-tuple-element.16) | data formatting | bytes 1048576

commit v3 on v2

--- a/solution.py
+++ b/solution.py
@@ -49,10 +49,10 @@
     fm_ref, corner_ref, hw_hbm, ow_ref, up_ref, first_ref, second_ref, map_ref,
     hw_ref, feat, far, row_all, col_all, weights, pooled, hid_acc,
     z_s, z_r, hd_own, hd_pair, hd_s, od_pair, od_s, hid_pair, s_flat, chunks, grads, map_acc, map_s, map_r,
-    za_s, za_r, yb_s, yb_r, ya_s, ya_r, zb_s, zb_r, x_s, x_r, c_s, c_r, gather,
+    za_s, za_r, yb_s, yb_r, ya_s, ya_r, zb_s, zb_r, x_s, x_r, c_s, c_r, t_ref, t_s1, t_r1, t_mid, t_s2, t_r2, t_s3, t_r3, t_all, t_far,
     acc_a, acc_b, mid_a, mid_b, final,
     hw_sem, f_sem, p_ss, p_rs, m_ss, m_rs,
-    za_ss, za_rs, yb_ss, yb_rs, ya_ss, ya_rs, zb_ss, zb_rs, xc_ss, xc_rs, g_ss, g_rs,
+    za_ss, za_rs, yb_ss, yb_rs, ya_ss, ya_rs, zb_ss, zb_rs, xc_ss, xc_rs, t_ss, t_rs,
 ):
     x, z, y, c = place()
     s = lax.axis_index("space")
@@ -99,9 +99,12 @@
     row_pick = (row_of == slot_at).astype(F32).astype(BF)
     col_pick = jnp.logical_and(spot - row_of * PITCH == slot_at, slot_at < COLS).astype(F32).astype(BF)
 
+    edges = corner_ref[...].astype(F32)
+    edges = jnp.transpose(jnp.concatenate([edges, edges], axis=0))
+
     def bins(low, high, grid, k):
-        start = corner_ref[:, low:low + 1].astype(F32)
-        size = (corner_ref[:, high:high + 1] - corner_ref[:, low:low + 1]).astype(F32) / POOL
+        start = edges[:, low:low + 1]
+        size = (edges[:, high:high + 1] - start) / POOL
         total = jnp.zeros((ROIS, 128), F32)
         for offset in (0.25, 0.75):
             point = start + (k + offset) * size - 0.5
@@ -180,9 +183,14 @@
     send_hid.wait_recv()
     send_od.wait_recv()
     second = lax.dot_general(hid_pair[...], od_pair[...], TN, preferred_element_type=F32)
-    for u in range(2):
-        chunks[u, :, :, 0:8, :] = second[:, u * 128:(u + 1) * 128].reshape(8, 4, 8, 128)
-        chunks[u, :, :, 200:208, :] = jnp.zeros((8, 4, 8, 128), F32)
+    chunks[:, :, :, 192:200, :] = jnp.zeros((2, 8, 4, 8, 128), F32)
+    t_ref[...] = second.reshape(4, 8, 8, 256)
+    t_s1[...] = t_ref[...].astype(BF)
+
+    def to_rows():
+        return [one(t_s1.at[(y + k) % 4], t_r1.at[k - 1], t_ss.at[k - 1], t_rs.at[k - 1], at_y(k)) for k in range(1, 4)]
+
+    rows_moved = to_rows()
     lax.fori_loop(0, POOL, wait_share, 0)
     send_hd.wait_recv()
 
@@ -195,7 +203,7 @@
     lax.fori_loop(0, POOL, weight_part, 0)
 
     def regroup(k, _):
-        chunks[k // 32, (k // 4) % 8, k % 4, 8:204, :] = s_flat[pl.ds(k * 196, 196)]
+        chunks[k // 32, (k // 4) % 8, k % 4, 0:196, :] = s_flat[pl.ds(k * 196, 196)]
         return 0
 
     lax.fori_loop(0, 64, regroup, 0)
@@ -234,10 +242,43 @@
 
         return go, total
 
-    za_go, za_total = ring(8, z, at_z, lambda u, d: chunks[u, d, :, 0:96, :], za_s, za_r, za_ss, za_rs)
-    yb_go, yb_total = ring(4, y, at_y, lambda u, d: chunks[u, :, d, 96:208, :], yb_s, yb_r, yb_ss, yb_rs)
+    za_go, za_total = ring(8, z, at_z, lambda u, d: chunks[u, d, :, 0:112, :], za_s, za_r, za_ss, za_rs)
+    yb_go, yb_total = ring(4, y, at_y, lambda u, d: chunks[u, :, d, 112:200, :], yb_s, yb_r, yb_ss, yb_rs)
     ya_go, ya_total = ring(4, y, at_y, lambda u, d: acc_a[u, d], ya_s, ya_r, ya_ss, ya_rs)
     zb_go, zb_total = ring(8, z, at_z, lambda u, d: acc_b[u, d], zb_s, zb_r, zb_ss, zb_rs)
+
+    def take_rows():
+        for copy in rows_moved:
+            copy.wait_recv()
+        t_mid[...] = t_ref[y] + (t_r1[0].astype(F32) + t_r1[1].astype(F32) + t_r1[2].astype(F32))
+        t_s2[...] = t_mid[...].astype(BF)
+        return [one(t_s2.at[(z + k) % 8], t_r2.at[k - 1], t_ss.at[k + 2], t_rs.at[k + 2], at_z(k)) for k in range(1, 8)]
+
+    def take_cells(moved):
+        for copy in moved:
+            copy.wait_recv()
+        total = t_mid[z]
+        for k in range(7):
+            total = total + t_r2[k].astype(F32)
+        t_s3[...] = total.astype(BF)
+        return one(t_s3, t_r3, t_ss.at[10], t_rs.at[10], at_x)
+
+    def take_pair(moved):
+        moved.wait_recv()
+        t_all[y, z] = (t_s3[...].astype(F32) + t_r3[...].astype(F32)).astype(BF)
+        mine = t_all.at[y, z]
+        return [one(mine, mine, t_ss.at[10 + k], t_rs.at[10 + k], at_z(k)) for k in range(1, 8)]
+
+    def spread_rows(moved):
+        for copy in moved:
+            copy.wait_recv()
+        mine = t_all.at[y]
+        return [one(mine, mine, t_ss.at[17 + k], t_rs.at[17 + k], at_y(k)) for k in range(1, 4)]
+
+    def spread_core(moved):
+        for copy in moved:
+            copy.wait_recv()
+        return one(t_all, t_far, t_ss.at[21], t_rs.at[21], at_c)
 
     def back_part(half):
         at = half * HALF
@@ -261,6 +302,7 @@
         za_go(k, 0)
     for k in (0, 1):
         yb_go(k, 0)
+    cells_moved = take_rows()
     for k in (2, 3):
         za_go(k, 0)
     for k in (2, 3):
@@ -271,54 +313,58 @@
         za_go(k, 1)
     for k in (0, 1):
         yb_go(k, 1)
+    pair_moved = take_cells(cells_moved)
     work(1, 3, 7)
     map_s[...] = jnp.transpose(map_acc[:, HALF:2 * HALF]).astype(BF)
     swap_map = one(map_s, map_r, m_ss.at[4], m_rs.at[4], at_s)
     for k in (0, 1, 2, 3):
         za_go(k, 2)
-    work(0, 0, 3)
-    for k in (0, 1):
-        za_go(k, 3)
+    cell_moved = take_pair(pair_moved)
     for u in (0, 1):
         acc_b[u] = yb_total(u)
         zb_go(u, 0)
     for k in (2, 3):
         zb_go(k, 0)
+    work(0, 0, 3)
+    for k in (0, 1):
+        za_go(k, 3)
+    for k in (0, 1, 2, 3):
+        zb_go(k, 1)
+    row_moved = spread_rows(cell_moved)
     work(0, 3, 7)
+    for k in (0, 1, 2, 3):
+        zb_go(k, 2)
     for u in (0, 1):
         acc_a[u] = za_total(u)
         ya_go(u, 0)
     for k in (2, 3):
         ya_go(k, 0)
-    for k in (0, 1, 2, 3):
-        zb_go(k, 1)
+    for k in (0, 1):
+        zb_go(k, 3)
+    core_moved = spread_core(row_moved)
+    near = jnp.transpose(map_acc[:, 0:HALF])
     for k in (0, 1):
         ya_go(k, 1)
-    for k in (0, 1, 2, 3):
-        zb_go(k, 2)
-    near = jnp.transpose(map_acc[:, 0:HALF])
-    for u in (0, 1):
-        mid_a[u] = ya_total(u)
-    for k in (0, 1):
-        zb_go(k, 3)
     swap_map.wait_recv()
     whole = near + map_r[...].astype(F32)
     for row in range(ROWS):
-        map_ref[row] = whole[row * PITCH:row * PITCH + COLS]
+        for k in range(2):
+            map_ref[pl.ds(row * 2 * COLS + k, COLS, stride=2), :] = whole[
+                row * PITCH:row * PITCH + COLS, k * 128:(k + 1) * 128
+            ]
     for u in (0, 1):
         mid_b[u] = zb_total(u)
-
-    x_s[0:96] = mid_a[1 - x].astype(BF)
-    x_s[96:208] = mid_b[1 - x].astype(BF)
+    for u in (0, 1):
+        mid_a[u] = ya_total(u)
+
+    x_s[0:112] = mid_a[1 - x].astype(BF)
+    x_s[112:200] = mid_b[1 - x].astype(BF)
     across = one(x_s, x_r, xc_ss.at[0], xc_rs.at[0], at_x)
     across.wait_recv()
-    final[0:96] = mid_a[x] + x_r[0:96].astype(F32)
-    final[96:208] = mid_b[x] + x_r[96:208].astype(F32)
-
-    gather[c, x, z, y] = final[0:8]
-    mine = gather.at[c, x, z, y]
-    steps = [one(mine, mine, g_ss.at[k], g_rs.at[k], at_z(k)) for k in range(1, 8)]
-    low, high = final[8:106], final[106:204]
+    final[0:112] = mid_a[x] + x_r[0:112].astype(F32)
+    final[112:200] = mid_b[x] + x_r[112:200].astype(F32)
+
+    low, high = final[0:98], final[98:196]
     c_s[...] = jnp.where(c == 0, high, low)
     swap = one(c_s, c_r, xc_ss.at[1], xc_rs.at[1], at_c)
     swap.wait_recv()
@@ -326,22 +372,11 @@
     got = c_r[...]
     first_ref[:, 0:128] = jnp.where(c == 0, kept, got)
     first_ref[:, 128:256] = jnp.where(c == 0, got, kept)
-    for step in steps:
-        step.wait_recv()
-    steps = []
-    for k in range(1, 4):
-        column = gather.at[c, x, :, y]
-        steps.append(one(column, column, g_ss.at[7 + k], g_rs.at[7 + k], at_y(k)))
-    for step in steps:
-        step.wait_recv()
-    plane = gather.at[c, x]
-    one(plane, plane, g_ss.at[11], g_rs.at[11], at_x).wait_recv()
-    half = gather.at[c]
-    one(half, half, g_ss.at[12], g_rs.at[12], at_c).wait_recv()
-    for k in range(2):
-        for u in range(2):
-            at = k * 256 + u * 128
-            second_ref[:, at:at + 128] = gather[k, u].reshape(256, 128)
+    core_moved.wait_recv()
+    here = t_all[...].astype(F32).reshape(256, 256)
+    there = t_far[...].astype(F32).reshape(256, 256)
+    second_ref[:, 0:256] = jnp.where(c == 0, here, there)
+    second_ref[:, 256:512] = jnp.where(c == 0, there, here)
     for copy in copies:
         copy.wait_send()
 
@@ -350,6 +385,12 @@
         return 0
 
     lax.fori_loop(0, POOL, sent, 0)
+
+
+def hand_over(first_ref, second_ref, map_ref, first_out, second_out, map_out):
+    first_out[...] = first_ref[...]
+    second_out[...] = second_ref[...]
+    map_out[...] = map_ref[...]
 
 
 def on_device(feature_map, proposals, hidden_weight, output_weight, upstream):
@@ -360,7 +401,7 @@
         out_shape=(
             jax.ShapeDtypeStruct((98, 256), F32),
             jax.ShapeDtypeStruct((256, 512), F32),
-            jax.ShapeDtypeStruct((ROWS, COLS, CHANNELS), F32),
+            jax.ShapeDtypeStruct((2 * ROWS * COLS, 128), F32),
         ),
         in_specs=[vmem, vmem, pl.BlockSpec(memory_space=pl.ANY), vmem, vmem],
         out_specs=[vmem] * 3,
@@ -379,30 +420,40 @@
             pltpu.VMEM((2 * ROIS, 256), BF), pltpu.VMEM((ROIS, 256), BF),
             pltpu.VMEM((2 * ROIS, 256), BF),
             pltpu.VMEM((POOL * WIDE, 128), F32),
-            pltpu.VMEM((2, 8, 4, 208, 128), F32),
+            pltpu.VMEM((2, 8, 4, 200, 128), F32),
             pltpu.VMEM((POOL, CHANNELS, BINS), BF),
             pltpu.VMEM((CHANNELS, 2 * HALF), F32),
             pltpu.VMEM((HALF, CHANNELS), BF), pltpu.VMEM((HALF, CHANNELS), BF),
-            pltpu.VMEM((14, 4, 96, 128), BF), pltpu.VMEM((14, 4, 96, 128), BF),
-            pltpu.VMEM((6, 8, 112, 128), BF), pltpu.VMEM((6, 8, 112, 128), BF),
-            pltpu.VMEM((6, 96, 128), BF), pltpu.VMEM((6, 96, 128), BF),
-            pltpu.VMEM((14, 112, 128), BF), pltpu.VMEM((14, 112, 128), BF),
-            pltpu.VMEM((208, 128), BF), pltpu.VMEM((208, 128), BF),
+            pltpu.VMEM((14, 4, 112, 128), BF), pltpu.VMEM((14, 4, 112, 128), BF),
+            pltpu.VMEM((6, 8, 88, 128), BF), pltpu.VMEM((6, 8, 88, 128), BF),
+            pltpu.VMEM((6, 112, 128), BF), pltpu.VMEM((6, 112, 128), BF),
+            pltpu.VMEM((14, 88, 128), BF), pltpu.VMEM((14, 88, 128), BF),
+            pltpu.VMEM((200, 128), BF), pltpu.VMEM((200, 128), BF),
             pltpu.VMEM((98, 128), F32), pltpu.VMEM((98, 128), F32),
-            pltpu.VMEM((2, 2, 8, 4, 8, 128), F32),
-            pltpu.VMEM((2, 4, 96, 128), F32), pltpu.VMEM((2, 8, 112, 128), F32),
-            pltpu.VMEM((2, 96, 128), F32), pltpu.VMEM((2, 112, 128), F32),
-            pltpu.VMEM((208, 128), F32),
+            pltpu.VMEM((4, 8, 8, 256), F32), pltpu.VMEM((4, 8, 8, 256), BF), pltpu.VMEM((3, 8, 8, 256), BF),
+            pltpu.VMEM((8, 8, 256), F32), pltpu.VMEM((8, 8, 256), BF), pltpu.VMEM((7, 8, 256), BF),
+            pltpu.VMEM((8, 256), BF), pltpu.VMEM((8, 256), BF),
+            pltpu.VMEM((4, 8, 8, 256), BF), pltpu.VMEM((4, 8, 8, 256), BF),
+            pltpu.VMEM((2, 4, 112, 128), F32), pltpu.VMEM((2, 8, 88, 128), F32),
+            pltpu.VMEM((2, 112, 128), F32), pltpu.VMEM((2, 88, 128), F32),
+            pltpu.VMEM((200, 128), F32),
             dma(()), dma((2,)), dma((POOL,)), dma((POOL,)), dma((5,)), dma((5,)),
             dma((14,)), dma((14,)), dma((6,)), dma((6,)), dma((6,)), dma((6,)), dma((14,)), dma((14,)),
-            dma((2,)), dma((2,)), dma((13,)), dma((13,)),
+            dma((2,)), dma((2,)), dma((22,)), dma((22,)),
         ],
         compiler_params=pltpu.CompilerParams(
             collective_id=1, has_side_effects=True, vmem_limit_bytes=67043328
         ),
         name="box_head_step",
-    )(feature_map[0], proposals[0], hidden_weight, output_weight, upstream[0])
-    return (first, second, grad[None])
+    )(feature_map[0], jnp.transpose(proposals[0]), hidden_weight, output_weight, upstream[0])
+    first, second, grad = pl.pallas_call(
+        hand_over,
+        out_shape=tuple(jax.ShapeDtypeStruct(v.shape, v.dtype) for v in (first, second, grad)),
+        in_specs=[vmem] * 3,
+        out_specs=[vmem] * 3,
+        name="hand_over",
+    )(first, second, grad)
+    return (first, second, grad.reshape(1, ROWS, COLS, CHANNELS))
 
 
 def solution(mesh):

time: 107 us -> 89.7 us (0.84)
  Pallas kernels: 98.5 us -> 88.9 us
  local copies, waits for them, and re-layouts: 8.09 us -> 0 us
    pallas_call x1, Pallas kernels: 98.5 us -> 86.3 us  [on_device(): pl.pallas_call(step_kernel, out_shape=(jax.ShapeDtypeStruct((98, 256), F3...]
    unnamed x4 -> x0, local copies, waits for them, and re-layouts: 8.09 us -> none
    pallas_call x0 -> x1, Pallas kernels: none -> 2.62 us  [on_device(): pl.pallas_call(hand_over, out_shape=tuple((jax.ShapeDtypeStruct(v.shape,...]
where the time goes in v3:
time: 89.7 us; the launch traced here: 89.6 us
  Pallas kernels  88.9 us (99%)
    pallas_call x1, Pallas kernels, on_device(): pl.pallas_call(step_kernel, out_shape=(jax.ShapeDtypeStruct((98, 256), F3...  86.3 us
    pallas_call x1, Pallas kernels, on_device(): pl.pallas_call(hand_over, out_shape=tuple((jax.ShapeDtypeStruct(v.shape,...  2.62 us

profile of v3, /device:TPU:1, one launch (start us, length us, event | category | flops | bytes accessed | tf_op | source)
XLA Modules:
  0.0 89.6 jit_solution(17441023788814409784)
XLA Ops:
  0.6 86.3 %box_head_step.1 = (f32[98,256]{1,0:T(8,128)}, f32[256,512]{1,0:T(8,128)}, f32[2016,128]{1,0:T(8,128)}) custom-call(bf16[12,84,256]{2,1,0:T(8,128)(2,1)} %bitcast.6, s32[4,128]{1,0:T(4,128)} %bitcast.8, bf16[12544,256]{1,0:T(8,128)(2,1)} %hw_hbm.1, bf16[256,512]{1,0:T(8,128)(2,1)} %ow_ref.1, bf16[128,512]{1,0:T(8,128)(2,1)} %bitcast.7), custom_call_target="tpu_custom_call" | custom-call | tf_op jit(solution)/shard_map/box_head_step/pallas_call | solution.py:399
  86.9 2.6 %hand_over.1 = (f32[98,256]{1,0:T(8,128)}, f32[256,512]{1,0:T(8,128)}, f32[2016,128]{1,0:T(8,128)}) custom-call(f32[98,256]{1,0:T(8,128)} %get-tuple-element.9.first_ref, f32[256,512]{1,0:T(8,128)} %get-tuple-element.10.second_ref, f32[2016,128]{1,0:T(8,128)} %get-tuple-element.11.map_ref), custom_call_target="tpu_custom_call" | custom-call | tf_op jit(solution)/shard_map/hand_over/pallas_call | solution.py:449

commit v4 on v3

--- a/solution.py
+++ b/solution.py
@@ -11,8 +11,9 @@
 CHANNELS = 256
 ROWS = 12
 COLS = 84
-PITCH = 96
-HALF = ROWS * PITCH
+CELLS = ROWS * COLS
+HALF = 1024
+FIRST = 768
 BINS = POOL * ROIS
 WIDE = POOL * CHANNELS
 BF = jnp.bfloat16
@@ -47,7 +48,7 @@
 
 def step_kernel(
     fm_ref, corner_ref, hw_hbm, ow_ref, up_ref, first_ref, second_ref, map_ref,
-    hw_ref, feat, far, row_all, col_all, weights, pooled, hid_acc,
+    hw_ref, feat, flat, row_all, col_all, weights, pooled, hid_acc,
     z_s, z_r, hd_own, hd_pair, hd_s, od_pair, od_s, hid_pair, s_flat, chunks, grads, map_acc, map_s, map_r,
     za_s, za_r, yb_s, yb_r, ya_s, ya_r, zb_s, zb_r, x_s, x_r, c_s, c_r, t_ref, t_s1, t_r1, t_mid, t_s2, t_r2, t_s3, t_r3, t_all, t_far,
     acc_a, acc_b, mid_a, mid_b, final,
@@ -73,7 +74,6 @@
     peers = [at_s, at_c] + [at_z(k) for k in range(1, 8)] + [at_y(k) for k in range(1, 4)] + [at_x]
     for peer in peers:
         pl.semaphore_signal(barrier, inc=1, device_id=peer, device_id_type=MESH)
-    pl.semaphore_wait(barrier, len(peers))
 
     copies = []
 
@@ -85,19 +85,21 @@
         copies.append(copy)
         return copy
 
-    features = one(fm_ref, far, f_sem.at[0], f_sem.at[1], at_s)
-
-    feat[...] = jnp.zeros((2 * HALF, CHANNELS), BF)
+    flat[CELLS:HALF] = jnp.zeros((HALF - CELLS, CHANNELS), F32)
     for row in range(ROWS):
-        feat[row * PITCH:row * PITCH + COLS] = fm_ref[row]
+        flat[row * COLS:(row + 1) * COLS] = fm_ref[row].astype(F32)
+    feat[0:HALF] = flat[...].astype(BF)
     lane = lax.broadcasted_iota(jnp.int32, (ROIS, 128), 1).astype(F32)
     base = (ROWS * s).astype(F32)
     row_at = jnp.where(lane < ROWS, lane + base, lane - base)
-    spot = lax.broadcasted_iota(jnp.int32, (128, 2 * HALF), 1).astype(F32)
-    slot_at = lax.broadcasted_iota(jnp.int32, (128, 2 * HALF), 0).astype(F32)
-    row_of = jnp.floor((spot + 0.5) * (1.0 / PITCH))
-    row_pick = (row_of == slot_at).astype(F32).astype(BF)
-    col_pick = jnp.logical_and(spot - row_of * PITCH == slot_at, slot_at < COLS).astype(F32).astype(BF)
+    spot = lax.broadcasted_iota(jnp.int32, (128, HALF), 1).astype(F32)
+    slot_at = lax.broadcasted_iota(jnp.int32, (128, HALF), 0).astype(F32)
+    row_of = jnp.floor((spot + 0.5) * (1.0 / COLS))
+    inside = spot < CELLS
+    row_pick = [
+        jnp.logical_and(row_of + first == slot_at, inside).astype(F32).astype(BF) for first in (0, ROWS)
+    ]
+    col_pick = jnp.logical_and(spot - row_of * COLS == slot_at, inside).astype(F32).astype(BF)
 
     edges = corner_ref[...].astype(F32)
     edges = jnp.transpose(jnp.concatenate([edges, edges], axis=0))
@@ -112,26 +114,46 @@
         return (0.5 * total).astype(BF)
 
     for k in range(POOL):
-        row_all[k] = jnp.dot(bins(0, 2, row_at, k), row_pick, preferred_element_type=F32).astype(BF)
+        rows = bins(0, 2, row_at, k)
+        for half in range(2):
+            row_all[k, :, half * HALF:(half + 1) * HALF] = jnp.dot(
+                rows, row_pick[half], preferred_element_type=F32
+            ).astype(BF)
         col_all[k] = jnp.dot(bins(1, 3, lane, k), col_pick, preferred_element_type=F32).astype(BF)
 
-    def build(i, half):
+    pl.semaphore_wait(barrier, len(peers))
+    features = [
+        one(feat.at[low:high], feat.at[HALF + low:HALF + high], f_sem.at[k], f_sem.at[2 + k], at_s)
+        for k, (low, high) in enumerate(((0, FIRST), (FIRST, HALF)))
+    ]
+
+    def build(i, half, low=0, high=HALF):
         at = half * HALF
         for j in range(POOL):
-            weights[j * ROIS:(j + 1) * ROIS, at:at + HALF] = col_all[j, :, at:at + HALF] * row_all[i, :, at:at + HALF]
-        return weights[:, at:at + HALF]
+            weights[j * ROIS:(j + 1) * ROIS, low:high] = (
+                col_all[j, :, low:high] * row_all[i, :, at + low:at + high]
+            )
+        return weights[:, low:high]
+
+    def held(i, k):
+        return pl.ds(pl.multiple_of((k * POOL + i) * BINS, BINS), BINS)
 
     def near_part(i, _):
         value = jnp.dot(build(i, 0), feat[0:HALF], preferred_element_type=F32)
         for k in range(2):
-            s_flat[pl.ds(pl.multiple_of((k * POOL + i) * BINS, BINS), BINS)] = value[:, k * 128:(k + 1) * 128]
+            s_flat[held(i, k)] = value[:, k * 128:(k + 1) * 128]
+        return 0
+
+    def far_first(i, _):
+        value = jnp.dot(build(i, 1, 0, FIRST), feat[HALF:HALF + FIRST], preferred_element_type=F32)
+        for k in range(2):
+            s_flat[held(i, k)] += value[:, k * 128:(k + 1) * 128]
         return 0
 
     lax.fori_loop(0, POOL, near_part, 0)
-    features.wait_recv()
-    for row in range(ROWS):
-        at = HALF + row * PITCH
-        feat[at:at + COLS] = far[row]
+    features[0].wait_recv()
+    lax.fori_loop(0, POOL, far_first, 0)
+    features[1].wait_recv()
     load_hw.wait()
     hid_acc[...] = jnp.zeros((ROIS, CHANNELS), F32)
 
@@ -142,8 +164,8 @@
         )
 
     def far_part(i, _):
-        value = jnp.dot(build(i, 1), feat[HALF:2 * HALF], preferred_element_type=F32)
-        near = [s_flat[pl.ds(pl.multiple_of((k * POOL + i) * BINS, BINS), BINS)] for k in range(2)]
+        value = jnp.dot(build(i, 1, FIRST, HALF), feat[HALF + FIRST:2 * HALF], preferred_element_type=F32)
+        near = [s_flat[held(i, k)] for k in range(2)]
         value = (value + jnp.concatenate(near, axis=1)).astype(BF)
         for j in range(POOL):
             pooled[i, 0:ROIS, j * CHANNELS:(j + 1) * CHANNELS] = value[j * ROIS:(j + 1) * ROIS]
@@ -183,7 +205,6 @@
     send_hid.wait_recv()
     send_od.wait_recv()
     second = lax.dot_general(hid_pair[...], od_pair[...], TN, preferred_element_type=F32)
-    chunks[:, :, :, 192:200, :] = jnp.zeros((2, 8, 4, 8, 128), F32)
     t_ref[...] = second.reshape(4, 8, 8, 256)
     t_s1[...] = t_ref[...].astype(BF)
 
@@ -203,7 +224,8 @@
     lax.fori_loop(0, POOL, weight_part, 0)
 
     def regroup(k, _):
-        chunks[k // 32, (k // 4) % 8, k % 4, 0:196, :] = s_flat[pl.ds(k * 196, 196)]
+        value = jnp.concatenate([s_flat[pl.ds(k * 196, 196)], jnp.zeros((4, 128), F32)], axis=0)
+        chunks[k // 32, (k // 4) % 8, k % 4] = value.astype(BF)
         return 0
 
     lax.fori_loop(0, 64, regroup, 0)
@@ -217,23 +239,16 @@
 
         def go(k, h):
             u, way, hops = chains[k]
+            at = slot(k, h)
+            source = own(u, (pos + way * (hops - h) + size) % size)
             if h > 0:
                 live[k, h - 1].wait_recv()
-            dest = (pos + way * (hops - h) + size) % size
-            value = own(u, dest)
-            if h > 0:
-                value = value + recv[slot(k, h - 1)].astype(F32)
-            at = slot(k, h)
-            send[at] = value.astype(BF)
-            live[k, h] = pltpu.make_async_remote_copy(
-                src_ref=send.at[at], dst_ref=recv.at[at], send_sem=ssem.at[at], recv_sem=rsem.at[at],
-                device_id=to(way), device_id_type=MESH,
-            )
-            live[k, h].start()
-            copies.append(live[k, h])
+                send[at] = source[...] + recv[at - 1]
+                source = send.at[at]
+            live[k, h] = one(source, recv.at[at], ssem.at[at], rsem.at[at], to(way))
 
         def total(u):
-            value = own(u, pos)
+            value = own(u, pos)[...].astype(F32)
             for k, (piece, _, hops) in enumerate(chains):
                 if piece == u and hops > 0:
                     live[k, hops - 1].wait_recv()
@@ -242,10 +257,10 @@
 
         return go, total
 
-    za_go, za_total = ring(8, z, at_z, lambda u, d: chunks[u, d, :, 0:112, :], za_s, za_r, za_ss, za_rs)
-    yb_go, yb_total = ring(4, y, at_y, lambda u, d: chunks[u, :, d, 112:200, :], yb_s, yb_r, yb_ss, yb_rs)
-    ya_go, ya_total = ring(4, y, at_y, lambda u, d: acc_a[u, d], ya_s, ya_r, ya_ss, ya_rs)
-    zb_go, zb_total = ring(8, z, at_z, lambda u, d: acc_b[u, d], zb_s, zb_r, zb_ss, zb_rs)
+    za_go, za_total = ring(8, z, at_z, lambda u, d: chunks.at[u, d, :, 0:112, :], za_s, za_r, za_ss, za_rs)
+    yb_go, yb_total = ring(4, y, at_y, lambda u, d: chunks.at[u, :, d, 112:200, :], yb_s, yb_r, yb_ss, yb_rs)
+    ya_go, ya_total = ring(4, y, at_y, lambda u, d: acc_a.at[u, d], ya_s, ya_r, ya_ss, ya_rs)
+    zb_go, zb_total = ring(8, z, at_z, lambda u, d: acc_b.at[u, d], zb_s, zb_r, zb_ss, zb_rs)
 
     def take_rows():
         for copy in rows_moved:
@@ -321,7 +336,7 @@
         za_go(k, 2)
     cell_moved = take_pair(pair_moved)
     for u in (0, 1):
-        acc_b[u] = yb_total(u)
+        acc_b[u] = yb_total(u).astype(BF)
         zb_go(u, 0)
     for k in (2, 3):
         zb_go(k, 0)
@@ -335,7 +350,7 @@
     for k in (0, 1, 2, 3):
         zb_go(k, 2)
     for u in (0, 1):
-        acc_a[u] = za_total(u)
+        acc_a[u] = za_total(u).astype(BF)
         ya_go(u, 0)
     for k in (2, 3):
         ya_go(k, 0)
@@ -347,11 +362,8 @@
         ya_go(k, 1)
     swap_map.wait_recv()
     whole = near + map_r[...].astype(F32)
-    for row in range(ROWS):
-        for k in range(2):
-            map_ref[pl.ds(row * 2 * COLS + k, COLS, stride=2), :] = whole[
-                row * PITCH:row * PITCH + COLS, k * 128:(k + 1) * 128
-            ]
+    for k in range(2):
+        map_ref[pl.ds(k, CELLS, stride=2), :] = whole[0:CELLS, k * 128:(k + 1) * 128]
     for u in (0, 1):
         mid_b[u] = zb_total(u)
     for u in (0, 1):
@@ -408,10 +420,10 @@
         scratch_shapes=[
             pltpu.VMEM((POOL * WIDE, 256), BF),
             pltpu.VMEM((2 * HALF, CHANNELS), BF),
-            pltpu.VMEM((ROWS, COLS, CHANNELS), BF),
+            pltpu.VMEM((HALF, CHANNELS), F32),
             pltpu.VMEM((POOL, ROIS, 2 * HALF), BF),
-            pltpu.VMEM((POOL, ROIS, 2 * HALF), BF),
-            pltpu.VMEM((BINS, 2 * HALF), BF),
+            pltpu.VMEM((POOL, ROIS, HALF), BF),
+            pltpu.VMEM((BINS, HALF), BF),
             pltpu.VMEM((POOL, 2 * ROIS, WIDE), BF),
             pltpu.VMEM((ROIS, CHANNELS), F32),
             pltpu.VMEM((ROIS, 512), BF), pltpu.VMEM((ROIS, 512), BF),
@@ -420,7 +432,7 @@
             pltpu.VMEM((2 * ROIS, 256), BF), pltpu.VMEM((ROIS, 256), BF),
             pltpu.VMEM((2 * ROIS, 256), BF),
             pltpu.VMEM((POOL * WIDE, 128), F32),
-            pltpu.VMEM((2, 8, 4, 200, 128), F32),
+            pltpu.VMEM((2, 8, 4, 200, 128), BF),
             pltpu.VMEM((POOL, CHANNELS, BINS), BF),
             pltpu.VMEM((CHANNELS, 2 * HALF), F32),
             pltpu.VMEM((HALF, CHANNELS), BF), pltpu.VMEM((HALF, CHANNELS), BF),
@@ -434,10 +446,10 @@
             pltpu.VMEM((8, 8, 256), F32), pltpu.VMEM((8, 8, 256), BF), pltpu.VMEM((7, 8, 256), BF),
             pltpu.VMEM((8, 256), BF), pltpu.VMEM((8, 256), BF),
             pltpu.VMEM((4, 8, 8, 256), BF), pltpu.VMEM((4, 8, 8, 256), BF),
-            pltpu.VMEM((2, 4, 112, 128), F32), pltpu.VMEM((2, 8, 88, 128), F32),
+            pltpu.VMEM((2, 4, 112, 128), BF), pltpu.VMEM((2, 8, 88, 128), BF),
             pltpu.VMEM((2, 112, 128), F32), pltpu.VMEM((2, 88, 128), F32),
             pltpu.VMEM((200, 128), F32),
-            dma(()), dma((2,)), dma((POOL,)), dma((POOL,)), dma((5,)), dma((5,)),
+            dma(()), dma((4,)), dma((POOL,)), dma((POOL,)), dma((5,)), dma((5,)),
             dma((14,)), dma((14,)), dma((6,)), dma((6,)), dma((6,)), dma((6,)), dma((14,)), dma((14,)),
             dma((2,)), dma((2,)), dma((22,)), dma((22,)),
         ],

time: 89.7 us -> 86.9 us (0.969)
  Pallas kernels: 88.9 us -> 86.2 us
    pallas_call x1, Pallas kernels: 86.3 us -> 83.5 us  [on_device(): pl.pallas_call(step_kernel, out_shape=(jax.ShapeDtypeStruct((98, 256), F3...]
where the time goes in v4:
time: 86.9 us; the launch traced here: 86.8 us
  Pallas kernels  86.2 us (99%)
    pallas_call x1, Pallas kernels, on_device(): pl.pallas_call(step_kernel, out_shape=(jax.ShapeDtypeStruct((98, 256), F3...  83.5 us
    pallas_call x1, Pallas kernels, on_device(): pl.pallas_call(hand_over, out_shape=tuple((jax.ShapeDtypeStruct(v.shape,...  2.62 us

profile of v4, /device:TPU:1, one launch (start us, length us, event | category | flops | bytes accessed | tf_op | source)
XLA Modules:
  0.0 86.8 jit_solution(13791231815579419167)
XLA Ops:
  0.6 83.5 %box_head_step.1 = (f32[98,256]{1,0:T(8,128)}, f32[256,512]{1,0:T(8,128)}, f32[2016,128]{1,0:T(8,128)}) custom-call(bf16[12,84,256]{2,1,0:T(8,128)(2,1)} %bitcast.6, s32[4,128]{1,0:T(4,128)} %bitcast.8, bf16[12544,256]{1,0:T(8,128)(2,1)} %hw_hbm.1, bf16[256,512]{1,0:T(8,128)(2,1)} %ow_ref.1, bf16[128,512]{1,0:T(8,128)(2,1)} %bitcast.7), custom_call_target="tpu_custom_call" | custom-call | tf_op jit(solution)/shard_map/box_head_step/pallas_call | solution.py:411
  84.2 2.6 %hand_over.1 = (f32[98,256]{1,0:T(8,128)}, f32[256,512]{1,0:T(8,128)}, f32[2016,128]{1,0:T(8,128)}) custom-call(f32[98,256]{1,0:T(8,128)} %get-tuple-element.9.first_ref, f32[256,512]{1,0:T(8,128)} %get-tuple-element.10.second_ref, f32[2016,128]{1,0:T(8,128)} %get-tuple-element.11.map_ref), custom_call_target="tpu_custom_call" | custom-call | tf_op jit(solution)/shard_map/hand_over/pallas_call | solution.py:461

commit v5 on v4

--- a/solution.py
+++ b/solution.py
@@ -50,10 +50,10 @@
     fm_ref, corner_ref, hw_hbm, ow_ref, up_ref, first_ref, second_ref, map_ref,
     hw_ref, feat, flat, row_all, col_all, weights, pooled, hid_acc,
     z_s, z_r, hd_own, hd_pair, hd_s, od_pair, od_s, hid_pair, s_flat, chunks, grads, map_acc, map_s, map_r,
-    za_s, za_r, yb_s, yb_r, ya_s, ya_r, zb_s, zb_r, x_s, x_r, c_s, c_r, t_ref, t_s1, t_r1, t_mid, t_s2, t_r2, t_s3, t_r3, t_all, t_far,
-    acc_a, acc_b, mid_a, mid_b, final,
+    za_s, za_r, yb_s, yb_r, ya_r, zb_r, q_s, q_r, t_ref, t_s1, t_r1, t_mid, t_s2, t_r2, t_s3, t_r3, t_all, t_far,
+    acc_a, acc_b, mid,
     hw_sem, f_sem, p_ss, p_rs, m_ss, m_rs,
-    za_ss, za_rs, yb_ss, yb_rs, ya_ss, ya_rs, zb_ss, zb_rs, xc_ss, xc_rs, t_ss, t_rs,
+    za_ss, za_rs, yb_ss, yb_rs, ya_ss, ya_rs, zb_ss, zb_rs, q_ss, q_rs, t_ss, t_rs,
 ):
     x, z, y, c = place()
     s = lax.axis_index("space")
@@ -66,12 +66,13 @@
 
     at_x = {"dp": index_of(1 - x, z, y, c)}
     at_c = {"dp": index_of(x, z, y, 1 - c)}
+    at_xc = {"dp": index_of(1 - x, z, y, 1 - c)}
     at_s = {"space": 1 - s}
 
     load_hw = pltpu.make_async_copy(hw_hbm, hw_ref, hw_sem)
     load_hw.start()
     barrier = pltpu.get_barrier_semaphore()
-    peers = [at_s, at_c] + [at_z(k) for k in range(1, 8)] + [at_y(k) for k in range(1, 4)] + [at_x]
+    peers = [at_s, at_c] + [at_z(k) for k in range(1, 8)] + [at_y(k) for k in range(1, 4)] + [at_x, at_xc]
     for peer in peers:
         pl.semaphore_signal(barrier, inc=1, device_id=peer, device_id_type=MESH)
 
@@ -221,14 +222,11 @@
         )
         return 0
 
-    lax.fori_loop(0, POOL, weight_part, 0)
-
     def regroup(k, _):
         value = jnp.concatenate([s_flat[pl.ds(k * 196, 196)], jnp.zeros((4, 128), F32)], axis=0)
         chunks[k // 32, (k // 4) % 8, k % 4] = value.astype(BF)
         return 0
 
-    lax.fori_loop(0, 64, regroup, 0)
 
     def ring(size, pos, to, own, send, recv, ssem, rsem):
         chains = chains_of(size // 2)
@@ -257,10 +255,27 @@
 
         return go, total
 
-    za_go, za_total = ring(8, z, at_z, lambda u, d: chunks.at[u, d, :, 0:112, :], za_s, za_r, za_ss, za_rs)
-    yb_go, yb_total = ring(4, y, at_y, lambda u, d: chunks.at[u, :, d, 112:200, :], yb_s, yb_r, yb_ss, yb_rs)
-    ya_go, ya_total = ring(4, y, at_y, lambda u, d: acc_a.at[u, d], ya_s, ya_r, ya_ss, ya_rs)
-    zb_go, zb_total = ring(8, z, at_z, lambda u, d: acc_b.at[u, d], zb_s, zb_r, zb_ss, zb_rs)
+    za_go, za_total = ring(8, z, at_z, lambda u, d: chunks.at[u, d, :, 0:96, :], za_s, za_r, za_ss, za_rs)
+    yb_go, yb_total = ring(4, y, at_y, lambda u, d: chunks.at[u, :, d, 96:200, :], yb_s, yb_r, yb_ss, yb_rs)
+    def direct(size, pos, to, acc, recv, ssem, rsem):
+        moved = {}
+
+        def go(u):
+            for k in range(1, size):
+                at = u * (size - 1) + k - 1
+                moved[u, k] = one(acc.at[u, (pos + k) % size], recv.at[at], ssem.at[at], rsem.at[at], to(k))
+
+        def total(u):
+            value = acc[u, pos].astype(F32)
+            for k in range(1, size):
+                moved[u, k].wait_recv()
+                value = value + recv[u * (size - 1) + k - 1].astype(F32)
+            return value
+
+        return go, total
+
+    ya_go, ya_total = direct(4, y, at_y, acc_a, ya_r, ya_ss, ya_rs)
+    zb_go, zb_total = direct(8, z, at_z, acc_b, zb_r, zb_ss, zb_rs)
 
     def take_rows():
         for copy in rows_moved:
@@ -313,77 +328,71 @@
     def work(half, low, high):
         lax.fori_loop(low, high, back_part(half), 0)
 
-    for k in (0, 1):
-        za_go(k, 0)
-    for k in (0, 1):
-        yb_go(k, 0)
+    lax.fori_loop(0, 4, weight_part, 0)
+    lax.fori_loop(0, 32, regroup, 0)
+    za_go(0, 0)
+    yb_go(0, 0)
+    za_go(2, 0)
+    yb_go(2, 0)
     cells_moved = take_rows()
-    for k in (2, 3):
-        za_go(k, 0)
-    for k in (2, 3):
-        yb_go(k, 0)
+    lax.fori_loop(4, POOL, weight_part, 0)
+    lax.fori_loop(32, 64, regroup, 0)
+    za_go(1, 0)
+    yb_go(1, 0)
+    za_go(3, 0)
     map_acc[...] = jnp.zeros((CHANNELS, 2 * HALF), F32)
-    work(1, 0, 3)
-    for k in (0, 1, 2, 3):
-        za_go(k, 1)
-    for k in (0, 1):
-        yb_go(k, 1)
+    za_go(0, 1)
+    za_go(2, 1)
+    work(1, 0, 1)
+    yb_go(0, 1)
+    yb_go(3, 0)
     pair_moved = take_cells(cells_moved)
-    work(1, 3, 7)
+    za_go(1, 1)
+    za_go(3, 1)
+    za_go(0, 2)
+    za_go(2, 2)
+    work(1, 1, 3)
+    yb_go(1, 1)
+    cell_moved = take_pair(pair_moved)
+    za_go(1, 2)
+    za_go(3, 2)
+    za_go(0, 3)
+    work(1, 3, 5)
+    acc_b[0] = yb_total(0).astype(BF)
+    zb_go(0)
+    za_go(1, 3)
+    row_moved = spread_rows(cell_moved)
+    work(1, 5, 7)
     map_s[...] = jnp.transpose(map_acc[:, HALF:2 * HALF]).astype(BF)
     swap_map = one(map_s, map_r, m_ss.at[4], m_rs.at[4], at_s)
-    for k in (0, 1, 2, 3):
-        za_go(k, 2)
-    cell_moved = take_pair(pair_moved)
-    for u in (0, 1):
-        acc_b[u] = yb_total(u).astype(BF)
-        zb_go(u, 0)
-    for k in (2, 3):
-        zb_go(k, 0)
-    work(0, 0, 3)
-    for k in (0, 1):
-        za_go(k, 3)
-    for k in (0, 1, 2, 3):
-        zb_go(k, 1)
-    row_moved = spread_rows(cell_moved)
-    work(0, 3, 7)
-    for k in (0, 1, 2, 3):
-        zb_go(k, 2)
+    acc_b[1] = yb_total(1).astype(BF)
+    zb_go(1)
     for u in (0, 1):
         acc_a[u] = za_total(u).astype(BF)
-        ya_go(u, 0)
-    for k in (2, 3):
-        ya_go(k, 0)
-    for k in (0, 1):
-        zb_go(k, 3)
+        ya_go(u)
     core_moved = spread_core(row_moved)
+    work(0, 0, 7)
     near = jnp.transpose(map_acc[:, 0:HALF])
-    for k in (0, 1):
-        ya_go(k, 1)
+    for u in (0, 1):
+        mid[u, 0:96] = ya_total(u)
+        mid[u, 96:200] = zb_total(u)
+    for u in (0, 1):
+        for k in (0, 1):
+            q_s[u, k] = mid[u, 98 * k:98 * k + 98].astype(BF)
+    ends = [
+        one(q_s.at[u, k], q_r.at[n], q_ss.at[n], q_rs.at[n], peer)
+        for n, (u, k, peer) in enumerate(((1 - x, c, at_x), (x, 1 - c, at_c), (1 - x, 1 - c, at_xc)))
+    ]
     swap_map.wait_recv()
     whole = near + map_r[...].astype(F32)
     for k in range(2):
         map_ref[pl.ds(k, CELLS, stride=2), :] = whole[0:CELLS, k * 128:(k + 1) * 128]
-    for u in (0, 1):
-        mid_b[u] = zb_total(u)
-    for u in (0, 1):
-        mid_a[u] = ya_total(u)
-
-    x_s[0:112] = mid_a[1 - x].astype(BF)
-    x_s[112:200] = mid_b[1 - x].astype(BF)
-    across = one(x_s, x_r, xc_ss.at[0], xc_rs.at[0], at_x)
-    across.wait_recv()
-    final[0:112] = mid_a[x] + x_r[0:112].astype(F32)
-    final[112:200] = mid_b[x] + x_r[112:200].astype(F32)
-
-    low, high = final[0:98], final[98:196]
-    c_s[...] = jnp.where(c == 0, high, low)
-    swap = one(c_s, c_r, xc_ss.at[1], xc_rs.at[1], at_c)
-    swap.wait_recv()
-    kept = jnp.where(c == 0, low, high)
-    got = c_r[...]
-    first_ref[:, 0:128] = jnp.where(c == 0, kept, got)
-    first_ref[:, 128:256] = jnp.where(c == 0, got, kept)
+    for copy in ends:
+        copy.wait_recv()
+    mine = q_s[x, c].astype(F32) + q_r[0].astype(F32)
+    others = q_r[1].astype(F32) + q_r[2].astype(F32)
+    first_ref[:, 0:128] = jnp.where(c == 0, mine, others)
+    first_ref[:, 128:256] = jnp.where(c == 0, others, mine)
     core_moved.wait_recv()
     here = t_all[...].astype(F32).reshape(256, 256)
     there = t_far[...].astype(F32).reshape(256, 256)
@@ -436,22 +445,20 @@
             pltpu.VMEM((POOL, CHANNELS, BINS), BF),
             pltpu.VMEM((CHANNELS, 2 * HALF), F32),
             pltpu.VMEM((HALF, CHANNELS), BF), pltpu.VMEM((HALF, CHANNELS), BF),
-            pltpu.VMEM((14, 4, 112, 128), BF), pltpu.VMEM((14, 4, 112, 128), BF),
-            pltpu.VMEM((6, 8, 88, 128), BF), pltpu.VMEM((6, 8, 88, 128), BF),
-            pltpu.VMEM((6, 112, 128), BF), pltpu.VMEM((6, 112, 128), BF),
-            pltpu.VMEM((14, 88, 128), BF), pltpu.VMEM((14, 88, 128), BF),
-            pltpu.VMEM((200, 128), BF), pltpu.VMEM((200, 128), BF),
-            pltpu.VMEM((98, 128), F32), pltpu.VMEM((98, 128), F32),
+            pltpu.VMEM((14, 4, 96, 128), BF), pltpu.VMEM((14, 4, 96, 128), BF),
+            pltpu.VMEM((6, 8, 104, 128), BF), pltpu.VMEM((6, 8, 104, 128), BF),
+            pltpu.VMEM((6, 96, 128), BF),
+            pltpu.VMEM((14, 104, 128), BF),
+            pltpu.VMEM((2, 2, 98, 128), BF), pltpu.VMEM((3, 98, 128), BF),
             pltpu.VMEM((4, 8, 8, 256), F32), pltpu.VMEM((4, 8, 8, 256), BF), pltpu.VMEM((3, 8, 8, 256), BF),
             pltpu.VMEM((8, 8, 256), F32), pltpu.VMEM((8, 8, 256), BF), pltpu.VMEM((7, 8, 256), BF),
             pltpu.VMEM((8, 256), BF), pltpu.VMEM((8, 256), BF),
             pltpu.VMEM((4, 8, 8, 256), BF), pltpu.VMEM((4, 8, 8, 256), BF),
-            pltpu.VMEM((2, 4, 112, 128), BF), pltpu.VMEM((2, 8, 88, 128), BF),
-            pltpu.VMEM((2, 112, 128), F32), pltpu.VMEM((2, 88, 128), F32),
-            pltpu.VMEM((200, 128), F32),
+            pltpu.VMEM((2, 4, 96, 128), BF), pltpu.VMEM((2, 8, 104, 128), BF),
+            pltpu.VMEM((2, 200, 128), F32),
             dma(()), dma((4,)), dma((POOL,)), dma((POOL,)), dma((5,)), dma((5,)),
             dma((14,)), dma((14,)), dma((6,)), dma((6,)), dma((6,)), dma((6,)), dma((14,)), dma((14,)),
-            dma((2,)), dma((2,)), dma((22,)), dma((22,)),
+            dma((3,)), dma((3,)), dma((22,)), dma((22,)),
         ],
         compiler_params=pltpu.CompilerParams(
             collective_id=1, has_side_effects=True, vmem_limit_bytes=67043328

time: 86.9 us -> 82.2 us (0.946)
  Pallas kernels: 86.2 us -> 81.4 us
    pallas_call x1, Pallas kernels: 83.5 us -> 78.8 us  [on_device(): pl.pallas_call(step_kernel, out_shape=(jax.ShapeDtypeStruct((98, 256), F3...]
where the time goes in v5:
time: 82.2 us; the launch traced here: 82 us
  Pallas kernels  81.4 us (99%)
    pallas_call x1, Pallas kernels, on_device(): pl.pallas_call(step_kernel, out_shape=(jax.ShapeDtypeStruct((98, 256), F3...  78.8 us
    pallas_call x1, Pallas kernels, on_device(): pl.pallas_call(hand_over, out_shape=tuple((jax.ShapeDtypeStruct(v.shape,...  2.62 us

profile of v5, /device:TPU:1, one launch (start us, length us, event | category | flops | bytes accessed | tf_op | source)
XLA Modules:
  0.0 82.0 jit_solution(4158813832443268646)
XLA Ops:
  0.6 78.8 %box_head_step.1 = (f32[98,256]{1,0:T(8,128)}, f32[256,512]{1,0:T(8,128)}, f32[2016,128]{1,0:T(8,128)}) custom-call(bf16[12,84,256]{2,1,0:T(8,128)(2,1)} %bitcast.6, s32[4,128]{1,0:T(4,128)} %bitcast.8, bf16[12544,256]{1,0:T(8,128)(2,1)} %hw_hbm.1, bf16[256,512]{1,0:T(8,128)(2,1)} %ow_ref.1, bf16[128,512]{1,0:T(8,128)(2,1)} %bitcast.7), custom_call_target="tpu_custom_call" | custom-call | tf_op jit(solution)/shard_map/box_head_step/pallas_call | solution.py:420
  79.4 2.6 %hand_over.1 = (f32[98,256]{1,0:T(8,128)}, f32[256,512]{1,0:T(8,128)}, f32[2016,128]{1,0:T(8,128)}) custom-call(f32[98,256]{1,0:T(8,128)} %get-tuple-element.9.first_ref, f32[256,512]{1,0:T(8,128)} %get-tuple-element.10.second_ref, f32[2016,128]{1,0:T(8,128)} %get-tuple-element.11.map_ref), custom_call_target="tpu_custom_call" | custom-call | tf_op jit(solution)/shard_map/hand_over/pallas_call | solution.py:468

commit v6 on v5

--- a/solution.py
+++ b/solution.py
@@ -14,6 +14,7 @@
 CELLS = ROWS * COLS
 HALF = 1024
 FIRST = 768
+EARLY = 3
 BINS = POOL * ROIS
 WIDE = POOL * CHANNELS
 BF = jnp.bfloat16
@@ -153,7 +154,7 @@
 
     lax.fori_loop(0, POOL, near_part, 0)
     features[0].wait_recv()
-    lax.fori_loop(0, POOL, far_first, 0)
+    lax.fori_loop(0, EARLY, far_first, 0)
     features[1].wait_recv()
     load_hw.wait()
     hid_acc[...] = jnp.zeros((ROIS, CHANNELS), F32)
@@ -164,19 +165,23 @@
             send_sem=p_ss.at[i], recv_sem=p_rs.at[i], device_id=at_c, device_id_type=MESH,
         )
 
-    def far_part(i, _):
-        value = jnp.dot(build(i, 1, FIRST, HALF), feat[HALF + FIRST:2 * HALF], preferred_element_type=F32)
-        near = [s_flat[held(i, k)] for k in range(2)]
-        value = (value + jnp.concatenate(near, axis=1)).astype(BF)
-        for j in range(POOL):
-            pooled[i, 0:ROIS, j * CHANNELS:(j + 1) * CHANNELS] = value[j * ROIS:(j + 1) * ROIS]
-        share(i).start()
-        hid_acc[...] += jnp.dot(
-            pooled[i, 0:ROIS], hw_ref[pl.ds(pl.multiple_of(i * WIDE, WIDE), WIDE)], preferred_element_type=F32
-        )
-        return 0
-
-    lax.fori_loop(0, POOL, far_part, 0)
+    def far_part(low):
+        def body(i, _):
+            value = jnp.dot(build(i, 1, low, HALF), feat[HALF + low:2 * HALF], preferred_element_type=F32)
+            near = [s_flat[held(i, k)] for k in range(2)]
+            value = (value + jnp.concatenate(near, axis=1)).astype(BF)
+            for j in range(POOL):
+                pooled[i, 0:ROIS, j * CHANNELS:(j + 1) * CHANNELS] = value[j * ROIS:(j + 1) * ROIS]
+            share(i).start()
+            hid_acc[...] += jnp.dot(
+                pooled[i, 0:ROIS], hw_ref[pl.ds(pl.multiple_of(i * WIDE, WIDE), WIDE)], preferred_element_type=F32
+            )
+            return 0
+
+        return body
+
+    lax.fori_loop(0, EARLY, far_part(FIRST), 0)
+    lax.fori_loop(EARLY, POOL, far_part(0), 0)
 
     pre_hidden = hid_acc[...]
     hidden = gelu_of(pre_hidden).astype(BF)
@@ -346,11 +351,11 @@
     work(1, 0, 1)
     yb_go(0, 1)
     yb_go(3, 0)
-    pair_moved = take_cells(cells_moved)
     za_go(1, 1)
     za_go(3, 1)
     za_go(0, 2)
     za_go(2, 2)
+    pair_moved = take_cells(cells_moved)
     work(1, 1, 3)
     yb_go(1, 1)
     cell_moved = take_pair(pair_moved)
@@ -383,6 +388,11 @@
         one(q_s.at[u, k], q_r.at[n], q_ss.at[n], q_rs.at[n], peer)
         for n, (u, k, peer) in enumerate(((1 - x, c, at_x), (x, 1 - c, at_c), (1 - x, 1 - c, at_xc)))
     ]
+    core_moved.wait_recv()
+    here = t_all[...].astype(F32).reshape(256, 256)
+    there = t_far[...].astype(F32).reshape(256, 256)
+    second_ref[:, 0:256] = jnp.where(c == 0, here, there)
+    second_ref[:, 256:512] = jnp.where(c == 0, there, here)
     swap_map.wait_recv()
     whole = near + map_r[...].astype(F32)
     for k in range(2):
@@ -393,11 +403,6 @@
     others = q_r[1].astype(F32) + q_r[2].astype(F32)
     first_ref[:, 0:128] = jnp.where(c == 0, mine, others)
     first_ref[:, 128:256] = jnp.where(c == 0, others, mine)
-    core_moved.wait_recv()
-    here = t_all[...].astype(F32).reshape(256, 256)
-    there = t_far[...].astype(F32).reshape(256, 256)
-    second_ref[:, 0:256] = jnp.where(c == 0, here, there)
-    second_ref[:, 256:512] = jnp.where(c == 0, there, here)
     for copy in copies:
         copy.wait_send()
 

time: 82.2 us -> 81.3 us (0.989)
  Pallas kernels: 81.4 us -> 80.5 us
    pallas_call x1, Pallas kernels: 78.8 us -> 77.9 us  [on_device(): pl.pallas_call(step_kernel, out_shape=(jax.ShapeDtypeStruct((98, 256), F3...]
where the time goes in v6:
time: 81.3 us; the launch traced here: 81.2 us
  Pallas kernels  80.5 us (99%)
    pallas_call x1, Pallas kernels, on_device(): pl.pallas_call(step_kernel, out_shape=(jax.ShapeDtypeStruct((98, 256), F3...  77.9 us
    pallas_call x1, Pallas kernels, on_device(): pl.pallas_call(hand_over, out_shape=tuple((jax.ShapeDtypeStruct(v.shape,...  2.62 us

profile of v6, /device:TPU:1, one launch (start us, length us, event | category | flops | bytes accessed | tf_op | source)
XLA Modules:
  0.0 81.2 jit_solution(4532173789148999089)
XLA Ops:
  0.6 77.9 %box_head_step.1 = (f32[98,256]{1,0:T(8,128)}, f32[256,512]{1,0:T(8,128)}, f32[2016,128]{1,0:T(8,128)}) custom-call(bf16[12,84,256]{2,1,0:T(8,128)(2,1)} %bitcast.6, s32[4,128]{1,0:T(4,128)} %bitcast.8, bf16[12544,256]{1,0:T(8,128)(2,1)} %hw_hbm.1, bf16[256,512]{1,0:T(8,128)(2,1)} %ow_ref.1, bf16[128,512]{1,0:T(8,128)(2,1)} %bitcast.7), custom_call_target="tpu_custom_call" | custom-call | tf_op jit(solution)/shard_map/box_head_step/pallas_call | solution.py:425
  78.6 2.6 %hand_over.1 = (f32[98,256]{1,0:T(8,128)}, f32[256,512]{1,0:T(8,128)}, f32[2016,128]{1,0:T(8,128)}) custom-call(f32[98,256]{1,0:T(8,128)} %get-tuple-element.9.first_ref, f32[256,512]{1,0:T(8,128)} %get-tuple-element.10.second_ref, f32[2016,128]{1,0:T(8,128)} %get-tuple-element.11.map_ref), custom_call_target="tpu_custom_call" | custom-call | tf_op jit(solution)/shard_map/hand_over/pallas_call | solution.py:473
